TPU v7x, 128 devices: a whole 4x4x4 slice. The times are simulated.
128 devices in a mesh: row: 8 (over x, y_lo), col: 16 (over y_hi, z, core).
Axes of the slice: x: 4, y: 4 (y_hi: 2, y_lo: 2; y = y_hi * 2 + y_lo), z: 4, core: 2. Of those that a mesh axis runs over, the one named last changes fastest.
Arguments:
- tokens: bfloat16 [16384, 2048], P(('row', 'col')), may hold values from -6 to 6
- norm_gain: float32 [2048], replicated, may hold values from 0.5 to 1.5
- router_weight: bfloat16 [2048, 64], P('row'), may hold values from -0.125 to 0.125
- expert_ids: int32 [16384, 3], P(('row', 'col')), may hold values from 0 to 63, all different within a row; in each aligned block of 128 rows (0 to 127, 128 to 255, ...) at most 8 rows name the same one
- w_gate: bfloat16 [128, 2048, 704], P(('row', 'col')), may hold values from -0.125 to 0.125
- w_up: bfloat16 [128, 2048, 704], P(('row', 'col')), may hold values from -0.125 to 0.125
- w_down: bfloat16 [128, 704, 2048], P(('row', 'col')), may hold values from -0.15625 to 0.15625
- grad_mixed: bfloat16 [16384, 2048], P(('row', 'col')), may hold values from -6 to 6
Outputs:
- mixed: bfloat16 [16384, 2048], P(('row', 'col'))
- grad_tokens: bfloat16 [16384, 2048], P(('row', 'col'))
- grad_gain: float32 [2048], replicated
- grad_router: float32 [2048, 64], P('row')
- grad_gate: bfloat16 [128, 2048, 704], P(('row', 'col'))
- grad_up: bfloat16 [128, 2048, 704], P(('row', 'col'))
- grad_down: bfloat16 [128, 704, 2048], P(('row', 'col'))
Inputs may be any that keep to these rules, and one draw needn't show every extreme that they name: `expert_ids`: each row names 3 different experts; in each aligned block of 128 rows (the tokens of one device) no expert is named by more than 8 rows, a bound that some block reaches.
All inputs are finite; a program needn't handle non-finite values.
Results may differ from a plain program's by a relative error of at most 0.0083.
Values may be sent and summed in bfloat16 or wider, within the bound.
No kernel may reach another device: no remote copies, remote signals or barrier semaphores. Data moves between devices by JAX's collectives and lax.ppermute only.
A program may use at most 128 MiB of HBM per device.

v0:
```python
import jax
import jax.numpy as jnp
from jax import lax
from jax.experimental import pallas as pl
from jax.experimental.pallas import tpu as pltpu
from jax.sharding import Mesh
from jax.sharding import PartitionSpec as P


ROW_COL = ("row_0", "row_1", "col_0", "col_1", "col_2")
CHIPS = ("row_0", "row_1", "col_0", "col_1")
ROW = ("row_0", "row_1")
CORE = "col_2"
CAP = 8
LANES = 128
F32 = jnp.float32
BF16 = jnp.bfloat16
EPSILON = 1e-06


def dot_nn(a, b):
    return lax.dot_general(a, b, (((1,), (0,)), ((), ())), preferred_element_type=F32)


def dot_nt(a, b):
    return lax.dot_general(a, b, (((1,), (1,)), ((), ())), preferred_element_type=F32)


def dot_tn(a, b):
    return lax.dot_general(a, b, (((0,), (0,)), ((), ())), preferred_element_type=F32)


def cost(flops, bytes_accessed):
    return pl.CostEstimate(flops=int(flops), bytes_accessed=int(bytes_accessed), transcendentals=0)


def whole(shape):
    return pl.BlockSpec(shape, lambda i: (0,) * len(shape))


def one_hot_rows(rows, cols, column_of):
    row = lax.broadcasted_iota(jnp.int32, (rows, cols), 0)
    col = lax.broadcasted_iota(jnp.int32, (rows, cols), 1)
    return jnp.where(column_of(row) == col, 1.0, 0.0).astype(BF16)


def dispatch_kernel(tok_ref, gain_ref, ids_ref, router_ref, send_ref, place_ref, scaled_scr):
    step = pl.program_id(0)
    chunks, tok_count, width = scaled_scr.shape
    slots = place_ref.shape[0]
    experts = slots // CAP

    @pl.when(step == 0)
    def _():
        x = tok_ref[...].astype(F32)
        inverse = lax.rsqrt(jnp.mean(x * x, axis=1, keepdims=True) + EPSILON)
        scaled = (x * inverse * gain_ref[...]).astype(BF16)
        for c in range(chunks):
            scaled_scr[c] = scaled[:, c * width : (c + 1) * width]
        ids = ids_ref[...]
        expert = lax.broadcasted_iota(jnp.int32, (experts, tok_count), 0)
        named = jnp.zeros((experts, tok_count), F32)
        for k in range(ids.shape[0]):
            named = named + jnp.where(ids[k : k + 1, :] == expert, 1.0, 0.0)
        before = lax.broadcasted_iota(jnp.int32, (tok_count, tok_count), 0)
        after = lax.broadcasted_iota(jnp.int32, (tok_count, tok_count), 1)
        earlier = jnp.where(before < after, 1.0, 0.0).astype(BF16)
        rank = dot_nn(named.astype(BF16), earlier)
        order = (named * (rank + 1.0)).astype(BF16)
        order_of = dot_nn(one_hot_rows(slots, experts, lambda row: row // CAP), order)
        want = (lax.broadcasted_iota(jnp.int32, (slots, tok_count), 0) % CAP + 1).astype(F32)
        place_ref[...] = jnp.where(order_of == want, 1.0, 0.0).astype(BF16)

    @pl.when(step < chunks)
    def _():
        send_ref[...] = dot_nn(place_ref[...], scaled_scr[jnp.minimum(step, chunks - 1)]).astype(BF16)

    @pl.when(step == chunks)
    def _():
        extra = jnp.zeros((slots, LANES), F32)
        for j in range(router_ref.shape[1] // LANES):
            pick = one_hot_rows(slots, experts, lambda row: jnp.where(row % CAP == j, row // CAP, -1))
            extra = extra + dot_nn(pick, router_ref[:, j * LANES : (j + 1) * LANES])
        send_ref[:, :LANES] = extra.astype(BF16)


def dispatch(tokens, gain, ids, router, slots):
    tok_count, width = tokens.shape
    chunks = 4
    part = width // chunks
    return pl.pallas_call(
        dispatch_kernel,
        grid=(chunks + 1,),
        out_shape=(
            jax.ShapeDtypeStruct((slots, width + LANES), BF16),
            jax.ShapeDtypeStruct((slots, tok_count), BF16),
        ),
        in_specs=[whole((tok_count, width)), whole((1, width)), whole(ids.shape), whole(router.shape)],
        out_specs=(
            pl.BlockSpec((slots, part), lambda i: (0, i)),
            whole((slots, tok_count)),
        ),
        scratch_shapes=[pltpu.VMEM((chunks, tok_count, part), BF16)],
        compiler_params=pltpu.CompilerParams(dimension_semantics=("arbitrary",)),
        cost_estimate=cost(2 * slots * tok_count * width, 2 * slots * width * 2),
        name="dispatch_tokens",
    )(tokens, gain, ids, router)


def column_kernel(extra_ref, rc_ref):
    extra = extra_ref[...].astype(F32)
    rows_n, per_row = 8, 2
    stride = extra.shape[0] // rows_n
    parts = [extra[r * stride + j : r * stride + j + 1, :] for r in range(rows_n) for j in range(per_row)]
    rc_ref[...] = jnp.broadcast_to(jnp.concatenate(parts, axis=1), rc_ref.shape).astype(BF16)


def own_column(rows_in, width):
    rows, _ = rows_in.shape
    return pl.pallas_call(
        column_kernel,
        grid=(1,),
        out_shape=jax.ShapeDtypeStruct((LANES, width), BF16),
        in_specs=[pl.BlockSpec((rows, LANES), lambda i: (0, width // LANES))],
        out_specs=whole((LANES, width)),
        cost_estimate=cost(rows * LANES, 2 * LANES * (rows + width)),
        name="own_column",
    )(rows_in)


def place_kernel(place_ref, x_ref, send_ref):
    send_ref[...] = dot_nn(place_ref[...], x_ref[...]).astype(BF16)


def place_rows(place, x):
    slots, tok_count = place.shape
    width = x.shape[1]
    chunks = 4
    part = width // chunks
    return pl.pallas_call(
        place_kernel,
        grid=(chunks,),
        out_shape=jax.ShapeDtypeStruct((slots, width), BF16),
        in_specs=[whole((slots, tok_count)), pl.BlockSpec((tok_count, part), lambda i: (0, i))],
        out_specs=pl.BlockSpec((slots, part), lambda i: (0, i)),
        compiler_params=pltpu.CompilerParams(dimension_semantics=("arbitrary",)),
        cost_estimate=cost(2 * slots * tok_count * width, 2 * slots * width * 2),
        name="dispatch_grads",
    )(place, x)


def forward_kernel(x_ref, wg_ref, wu_ref, wd_ref, rc_ref, out_ref, hg_ref, g_ref, u_ref, gate_ref):
    x = x_ref[...]
    gate = jax.nn.sigmoid(dot_nt(x, rc_ref[...]))
    g = dot_nt(x, wg_ref[...])
    u = dot_nt(x, wu_ref[...])
    hidden = g * jax.nn.sigmoid(g) * u
    gated = (hidden * gate[:, :1]).astype(BF16)
    out_ref[...] = dot_nn(gated, wd_ref[...]).astype(BF16)
    hg_ref[...] = gated
    g_ref[...] = g
    u_ref[...] = u
    gate_ref[...] = gate


def forward(x, wg, wu, wd, rc):
    rows = x.shape[0]
    ff, width = wg.shape
    blk = 256
    row_blk = lambda n: pl.BlockSpec((blk, n), lambda i: (i, 0))
    return pl.pallas_call(
        forward_kernel,
        grid=(rows // blk,),
        out_shape=(
            jax.ShapeDtypeStruct((rows, width), BF16),
            jax.ShapeDtypeStruct((rows, ff), BF16),
            jax.ShapeDtypeStruct((rows, ff), F32),
            jax.ShapeDtypeStruct((rows, ff), F32),
            jax.ShapeDtypeStruct((rows, LANES), F32),
        ),
        in_specs=[row_blk(width), whole((ff, width)), whole((ff, width)), whole((ff, width)), whole((LANES, width))],
        out_specs=(row_blk(width), row_blk(ff), row_blk(ff), row_blk(ff), row_blk(LANES)),
        compiler_params=pltpu.CompilerParams(dimension_semantics=("arbitrary",)),
        cost_estimate=cost(6 * rows * ff * width, 6 * ff * width + 8 * rows * width),
        name="expert_forward",
    )(x, wg, wu, wd, rc)


def backward_kernel(gr_ref, g_ref, u_ref, gate_ref, wg_ref, wu_ref, wd_ref, back_ref, dg_ref, du_ref, gg_ref):
    g = g_ref[...]
    u = u_ref[...]
    s = jax.nn.sigmoid(g)
    act = g * s
    dh = dot_nt(gr_ref[...], wd_ref[...])
    inner = jnp.sum(dh * (act * u), axis=1, keepdims=True)
    gg_ref[...] = jnp.broadcast_to(inner, gg_ref.shape)
    dh = dh * gate_ref[:, :1]
    dg = (dh * u * s * (1.0 + g * (1.0 - s))).astype(BF16)
    du = (dh * act).astype(BF16)
    dg_ref[...] = dg
    du_ref[...] = du
    back_ref[...] = (dot_nn(dg, wg_ref[...]) + dot_nn(du, wu_ref[...])).astype(BF16)


def backward(gr, g, u, gate, wg, wu, wd):
    rows, width = gr.shape
    ff = wg.shape[0]
    blk = 256
    row_blk = lambda n: pl.BlockSpec((blk, n), lambda i: (i, 0))
    return pl.pallas_call(
        backward_kernel,
        grid=(rows // blk,),
        out_shape=(
            jax.ShapeDtypeStruct((rows, width), BF16),
            jax.ShapeDtypeStruct((rows, ff), BF16),
            jax.ShapeDtypeStruct((rows, ff), BF16),
            jax.ShapeDtypeStruct((rows, LANES), F32),
        ),
        in_specs=[row_blk(width), row_blk(ff), row_blk(ff), row_blk(LANES)] + [whole((ff, width))] * 3,
        out_specs=(row_blk(width), row_blk(ff), row_blk(ff), row_blk(LANES)),
        compiler_params=pltpu.CompilerParams(dimension_semantics=("arbitrary",)),
        cost_estimate=cost(6 * rows * ff * width, 6 * ff * width + 8 * rows * width),
        name="expert_backward",
    )(gr, g, u, gate, wg, wu, wd)


def join_out_kernel(mine_ref, sib_ref, out_ref):
    out_ref[...] = (mine_ref[...].astype(F32) + sib_ref[...].astype(F32)).astype(BF16)


def join_halves(mine, sib):
    rows, width = mine.shape
    blk = pl.BlockSpec((128, width), lambda i: (i, 0))
    return pl.pallas_call(
        join_out_kernel,
        grid=(rows // 128,),
        out_shape=jax.ShapeDtypeStruct((rows, width), BF16),
        in_specs=[blk, blk],
        out_specs=blk,
        compiler_params=pltpu.CompilerParams(dimension_semantics=("arbitrary",)),
        cost_estimate=cost(3 * rows * width, 6 * rows * width),
        name="join_halves",
    )(mine, sib)


def weight_grad_kernel(d0_ref, d1_ref, x0_ref, x1_ref, out_ref):
    out_ref[...] = (dot_tn(d0_ref[...], x0_ref[...]) + dot_tn(d1_ref[...], x1_ref[...])).astype(BF16)


def weight_grad(d0, d1, x0, x1, width):
    rows, ff = d0.shape
    part = 512
    col = pl.BlockSpec((rows, part), lambda i: (0, i))
    return pl.pallas_call(
        weight_grad_kernel,
        grid=(width // part,),
        out_shape=jax.ShapeDtypeStruct((ff, width), BF16),
        in_specs=[whole((rows, ff)), whole((rows, ff)), col, col],
        out_specs=pl.BlockSpec((ff, part), lambda i: (0, i)),
        compiler_params=pltpu.CompilerParams(dimension_semantics=("arbitrary",)),
        cost_estimate=cost(4 * rows * ff * width, 4 * rows * width + 2 * ff * width),
    )(d0, d1, x0, x1)


def join_kernel(mine_ref, sib_ref, gg_ref, gg_sib_ref, gate_ref, rc_ref, x_ref, back_ref, gain_scr, router_scr):
    step = pl.program_id(0)
    chunks, _, part = gain_scr.shape
    rows = back_ref.shape[0]

    @pl.when(step < chunks)
    def _():
        c = jnp.minimum(step, chunks - 1)
        gate = gate_ref[...]
        gl = ((gg_ref[...] + gg_sib_ref[...]) * gate * (1.0 - gate)).astype(BF16).astype(F32)[:, :1]
        x = x_ref[...].astype(F32)
        back = mine_ref[...].astype(F32) + sib_ref[...].astype(F32) + gl * rc_ref[:1, :].astype(F32)
        back_ref[...] = back.astype(BF16)
        gain_scr[c] = jnp.sum(x * back, axis=0, keepdims=True)
        router_scr[c] = jnp.sum(x * gl, axis=0, keepdims=True)

    @pl.when(step == chunks)
    def _():
        lanes = chunks * part // CAP
        gain = jnp.concatenate([gain_scr[c] for c in range(chunks)], axis=1)
        gain = jnp.concatenate([gain[:, j * lanes : (j + 1) * lanes] for j in range(CAP)], axis=0)
        gain = jnp.broadcast_to(gain[None], (rows // CAP, CAP, lanes)).reshape(rows, lanes)
        back_ref[:, :lanes] = gain.astype(BF16)
        router = jnp.concatenate([router_scr[c] for c in range(chunks)], axis=1)
        parts = chunks * part // LANES
        router = jnp.concatenate([router[:, j * LANES : (j + 1) * LANES] for j in range(parts)], axis=0)
        per_row = parts // 8
        pick = one_hot_rows(
            rows,
            parts,
            lambda row: jnp.where(row % CAP < per_row, row // (rows // 8) * per_row + row % CAP, -1),
        )
        back_ref[:, lanes : lanes + LANES] = dot_nn(pick, router.astype(BF16)).astype(BF16)


def join_back(mine, sib, gg, gg_sib, gate, rc, x):
    rows, width = mine.shape
    part = 512
    chunks = width // part
    at = lambda i: (0, jnp.minimum(i, chunks - 1))
    col = pl.BlockSpec((rows, part), at)
    return pl.pallas_call(
        join_kernel,
        grid=(chunks + 1,),
        out_shape=jax.ShapeDtypeStruct((rows, width + width // CAP + LANES), BF16),
        in_specs=[col, col] + [whole((rows, LANES))] * 3 + [pl.BlockSpec((LANES, part), at), col],
        out_specs=pl.BlockSpec((rows, part), lambda i: (0, i)),
        scratch_shapes=[pltpu.VMEM((chunks, 1, part), F32), pltpu.VMEM((chunks, 1, part), F32)],
        compiler_params=pltpu.CompilerParams(dimension_semantics=("arbitrary",)),
        cost_estimate=cost(10 * rows * width, 8 * rows * width),
        name="join_back",
    )(mine, sib, gg, gg_sib, gate, rc, x)


def collect_kernel(a_ref, b_ref, c_ref, out_ref):
    rows = a_ref.shape[0]
    chips = rows // CAP
    for half, ref in enumerate((a_ref, b_ref)):
        total = jnp.sum(ref[...].astype(F32).reshape(chips, CAP, LANES), axis=0)
        out_ref[:CAP, half * LANES : (half + 1) * LANES] = total
    for j in range(2):
        pick = one_hot_rows(chips, rows, lambda row: row * CAP + j)
        out_ref[CAP:, j * LANES : (j + 1) * LANES] = dot_nn(pick, c_ref[...])


def collect(rows_in, width):
    rows = rows_in.shape[0]
    first = width // LANES
    lane = lambda k: pl.BlockSpec((rows, LANES), lambda i: (0, first + k))
    return pl.pallas_call(
        collect_kernel,
        grid=(1,),
        out_shape=jax.ShapeDtypeStruct((CAP + rows // CAP, 2 * LANES), F32),
        in_specs=[lane(0), lane(1), lane(2)],
        out_specs=whole((CAP + rows // CAP, 2 * LANES)),
        cost_estimate=cost(rows * rows * LANES, 6 * rows * LANES),
        name="collect_sums",
    )(rows_in, rows_in, rows_in)


def mix_kernel(place_ref, rows_ref, tok_ref, mixed_ref, acc_ref):
    step = pl.program_id(0)
    part = dot_tn(place_ref[...], rows_ref[...])

    @pl.when(step == 0)
    def _():
        acc_ref[...] = part

    @pl.when(step > 0)
    def _():
        acc_ref[...] += part

    @pl.when(step == pl.num_programs(0) - 1)
    def _():
        mixed_ref[...] = (tok_ref[...].astype(F32) + acc_ref[...]).astype(BF16)


def mix(place, rows, tokens):
    slots, tok_count = place.shape
    width = tokens.shape[1]
    part = 128
    return pl.pallas_call(
        mix_kernel,
        grid=(slots // part,),
        out_shape=jax.ShapeDtypeStruct((tok_count, width), BF16),
        in_specs=[
            pl.BlockSpec((part, tok_count), lambda i: (i, 0)),
            pl.BlockSpec((part, width), lambda i: (i, 0)),
            whole((tok_count, width)),
        ],
        out_specs=whole((tok_count, width)),
        scratch_shapes=[pltpu.VMEM((tok_count, width), F32)],
        compiler_params=pltpu.CompilerParams(dimension_semantics=("arbitrary",)),
        cost_estimate=cost(2 * slots * tok_count * width, 2 * slots * width),
        name="mix_outputs",
    )(place, rows, tokens)


def finish_kernel(place_ref, rows_ref, tok_ref, gain_ref, up_ref, out_ref, acc_ref):
    step = pl.program_id(0)
    part = dot_tn(place_ref[...], rows_ref[...])

    @pl.when(step == 0)
    def _():
        acc_ref[...] = part

    @pl.when(step > 0)
    def _():
        acc_ref[...] += part

    @pl.when(step == pl.num_programs(0) - 1)
    def _():
        x = tok_ref[...].astype(F32)
        inverse = lax.rsqrt(jnp.mean(x * x, axis=1, keepdims=True) + EPSILON)
        normed = x * inverse
        gn = acc_ref[...] * gain_ref[...]
        out = up_ref[...].astype(F32) + inverse * (gn - normed * jnp.mean(gn * normed, axis=1, keepdims=True))
        out_ref[...] = out.astype(BF16)


def finish(place, rows, tokens, gain, upstream):
    slots, tok_count = place.shape
    width = tokens.shape[1]
    part = 128
    return pl.pallas_call(
        finish_kernel,
        grid=(slots // part,),
        out_shape=jax.ShapeDtypeStruct((tok_count, width), BF16),
        in_specs=[
            pl.BlockSpec((part, tok_count), lambda i: (i, 0)),
            pl.BlockSpec((part, width), lambda i: (i, 0)),
            whole((tok_count, width)),
            whole((1, width)),
            whole((tok_count, width)),
        ],
        out_specs=whole((tok_count, width)),
        scratch_shapes=[pltpu.VMEM((tok_count, width), F32)],
        compiler_params=pltpu.CompilerParams(dimension_semantics=("arbitrary",)),
        cost_estimate=cost(2 * slots * tok_count * width, 2 * slots * width),
        name="finish_tokens",
    )(place, rows, tokens, gain, upstream)


def across(block, axis, bit):
    count = lax.axis_size(axis)
    return lax.ppermute(block, axis, [(i, i ^ bit) for i in range(count)])


def exchange(x, experts):
    rows, width = x.shape
    return lax.all_to_all(x.reshape(experts, -1, width), CHIPS, 0, 0, tiled=True).reshape(rows, width)


def local(tokens, norm_gain, router_weight, expert_ids, w_gate, w_up, w_down, grad_mixed):
    _, width = tokens.shape
    experts = router_weight.shape[1]
    slots = experts * CAP
    gain = norm_gain.reshape(1, width)
    wg, wu, wd = w_gate[0].T, w_up[0].T, w_down[0]

    send_in, place = dispatch(tokens, gain, expert_ids.T, router_weight.T, slots)
    in_0 = exchange(send_in, experts)
    rc = own_column(in_0, width)
    send_grad = place_rows(place, grad_mixed)
    gr_0 = exchange(send_grad, experts)
    in_1 = across(in_0, CORE, 1)
    gr_1 = across(gr_0, CORE, 1)

    out_0, hg_0, g_0, u_0, gate_0 = forward(in_0, wg, wu, wd, rc)
    out_1, hg_1, g_1, u_1, gate_1 = forward(in_1, wg, wu, wd, rc)
    out_s = across(out_1, CORE, 1)
    out = join_halves(out_0, out_s)
    got_out = exchange(out, experts)
    mixed = mix(place, got_out, tokens)

    back_0, dg_0, du_0, gg_0 = backward(gr_0, g_0, u_0, gate_0, wg, wu, wd)
    back_1, dg_1, du_1, gg_1 = backward(gr_1, g_1, u_1, gate_1, wg, wu, wd)
    back_s = across(back_1, CORE, 1)
    gg_s = across(gg_1, CORE, 1)
    back = join_back(back_0, back_s, gg_0, gg_s, gate_0, rc, in_0)
    got_back = exchange(back, experts)
    grad_tokens = finish(place, got_back, tokens, gain, grad_mixed)

    grad_down = weight_grad(hg_0, hg_1, gr_0, gr_1, width)
    grad_gate = weight_grad(dg_0, dg_1, in_0, in_1, width)
    grad_up = weight_grad(du_0, du_1, in_0, in_1, width)

    sums = collect(got_back, width)
    sums = sums + across(sums, CORE, 1)
    grad_gain = sums[:CAP].reshape(width) / norm_gain
    grad_router = sums[CAP:].T
    return (
        mixed,
        grad_tokens,
        grad_gain,
        grad_router,
        grad_gate.T[None],
        grad_up.T[None],
        grad_down[None],
    )


def solution(mesh):
    finer = Mesh(mesh.devices.reshape(4, 2, 2, 4, 2), ROW_COL)
    placed = (
        P(ROW_COL, None),
        P(),
        P(ROW, None),
        P(ROW_COL, None),
        P(ROW_COL, None, None),
        P(ROW_COL, None, None),
        P(ROW_COL, None, None),
        P(ROW_COL, None),
    )
    return jax.shard_map(
        local,
        mesh=finer,
        in_specs=placed,
        out_specs=(
            P(ROW_COL, None),
            P(ROW_COL, None),
            P(),
            P(ROW, None),
            P(ROW_COL, None, None),
            P(ROW_COL, None, None),
            P(ROW_COL, None, None),
        ),
        check_vma=False,
    )
```

profile of v0, /device:TPU:1, one launch (start us, length us, event | category | flops | bytes accessed | tf_op | source)
XLA Modules:
  0.0 229.4 jit_solution(7358989957523625325)
XLA Ops:
  0.6 4.6 %dispatch_tokens.1 = (bf16[512,2176]{1,0:T(8,128)(2,1)}, bf16[512,128]{1,0:T(8,128)(2,1)}) custom-call(bf16[128,2048]{1,0:T(8,128)(2,1)} %tok_ref.5, f32[1,2048]{1,0:T(1,128)} %bitcast.44, s32[3,128]{1,0:T(4,128)} %bitcast.60, bf16[64,256]{1,0:T(8,128)(2,1)} %bitcast.59), custom_call_target="tpu_custom_call" | custom-call | flops 268435456 | bytes 4194304 | tf_op jit(solution)/shard_map/dispatch_tokens/pallas_call | solution.py:91
  5.2 11.9 %all-to-all-start = ((bf16[64,8,2176]{2,1,0:T(8,128)(2,1)}), bf16[64,8,2176]{2,1,0:T(8,128)(2,1)S(1)}, u32[]{:S(2)}, u32[]{:S(2)}) async-start(bf16[64,8,2176]{2,1,0:T(8,128)(2,1)} %bitcast.43), calls=%async_computation | async-start | bytes 4456448 | tf_op jit(solution)/shard_map/all_to_all | solution.py:435
  17.2 4.0 %dispatch_grads.1 = bf16[512,2048]{1,0:T(8,128)(2,1)} custom-call(bf16[512,128]{1,0:T(8,128)(2,1)} %get-tuple-element.27.place_ref, bf16[128,2048]{1,0:T(8,128)(2,1)} %up_ref.1), custom_call_target="tpu_custom_call" | custom-call | flops 268435456 | bytes 4194304 | tf_op jit(solution)/shard_map/dispatch_grads/pallas_call | solution.py:140
  21.2 24.7 %all-to-all-done = bf16[64,8,2176]{2,1,0:T(8,128)(2,1)S(1)} async-done(((bf16[64,8,2176]{2,1,0:T(8,128)(2,1)}), bf16[64,8,2176]{2,1,0:T(8,128)(2,1)S(1)}, u32[]{:S(2)}, u32[]{:S(2)}) %all-to-all-start) | async-done | bytes 2228256 | tf_op jit(solution)/shard_map/all_to_all | solution.py:435
  45.9 7.8 %all-to-all-start.2 = ((bf16[64,8,2048]{2,1,0:T(8,128)(2,1)}), bf16[64,8,2048]{2,1,0:T(8,128)(2,1)}, u32[]{:S(2)}, u32[]{:S(2)}) async-start(bf16[64,8,2048]{2,1,0:T(8,128)(2,1)} %bitcast.42), calls=%async_computation.2 | async-start | bytes 4194304 | tf_op jit(solution)/shard_map/all_to_all | solution.py:435
  53.7 2.4 %collective-permute-start = (bf16[512,2176]{1,0:T(8,128)(2,1)S(1)}, bf16[512,2176]{1,0:T(8,128)(2,1)}, u32[]{:S(2)}, u32[]{:S(2)}) collective-permute-start(bf16[512,2176]{1,0:T(8,128)(2,1)S(1)} %bitcast.34), channel_id=1, source_target_pairs={{0,1},{1,0},{2,3},{3,2},{4,5},{5,4},{6,7},{7,6},{8,9},{9,8},{10,11... | collective-permute-start | bytes 6684680 | tf_op jit(solution)/shard_map/ppermute | solution.py:430
  56.1 23.4 %all-to-all-done.2 = bf16[64,8,2048]{2,1,0:T(8,128)(2,1)} async-done(((bf16[64,8,2048]{2,1,0:T(8,128)(2,1)}), bf16[64,8,2048]{2,1,0:T(8,128)(2,1)}, u32[]{:S(2)}, u32[]{:S(2)}) %all-to-all-start.2) | async-done | bytes 2097184 | tf_op jit(solution)/shard_map/all_to_all | solution.py:435
  79.5 4.3 %collective-permute-start.2 = (bf16[512,2048]{1,0:T(8,128)(2,1)}, bf16[512,2048]{1,0:T(8,128)(2,1)}, u32[]{:S(2)}, u32[]{:S(2)}) collective-permute-start(bf16[512,2048]{1,0:T(8,128)(2,1)} %bitcast.15.gr_ref.x0_ref), channel_id=1, source_target_pairs={{0,1},{1,0},{2,3},{3,2},{4,5},{5,4},{6,7},{7,6},{8,9},{9,8},{10,11... | collective-permute-start | bytes 6291464 | tf_op jit(solution)/shard_map/ppermute | solution.py:430
  85.6 11.5 %expert_forward.3 = (bf16[512,2048]{1,0:T(8,128)(2,1)}, bf16[512,704]{1,0:T(8,128)(2,1)}, f32[512,704]{1,0:T(8,128)}, f32[512,704]{1,0:T(8,128)}, f32[512,128]{1,0:T(8,128)}) custom-call(bf16[512,2176]{1,0:T(8,128)(2,1)} %collective-permute-done.x_ref.x1_ref, bf16[704,2048]{1,0:T(8,128)(2,1)} %bitcast.47, bf16[704,2048]{1,0:T(8,128)(2,1)} %bitcast.51, ...), custom_call_target="tpu_custom_call" | custom-call | flops 4429185024 | bytes 17039360 | tf_op jit(solution)/shard_map/expert_forward/pallas_call | solution.py:171
  97.1 12.6 %expert_backward.3 = (bf16[512,2048]{1,0:T(8,128)(2,1)}, bf16[512,704]{1,0:T(8,128)(2,1)}, bf16[512,704]{1,0:T(8,128)(2,1)}, f32[512,128]{1,0:T(8,128)}) custom-call(bf16[512,2048]{1,0:T(8,128)(2,1)} %collective-permute-done.2.gr_ref.x1_ref, f32[512,704]{1,0:T(8,128)} %get-tuple-element.35.g_ref, f32[512,704]{1,0:T(8,128)} %get-tuple-element.36.u_ref, ...), custom_call_target="tpu_custom_call" | custom-call | flops 4429185024 | bytes 17039360 | tf_op jit(solution)/shard_map/expert_backward/pallas_call | solution.py:210
  109.8 11.5 %expert_forward.2 = (bf16[512,2048]{1,0:T(8,128)(2,1)}, bf16[512,704]{1,0:T(8,128)(2,1)}, f32[512,704]{1,0:T(8,128)}, f32[512,704]{1,0:T(8,128)}, f32[512,128]{1,0:T(8,128)}) custom-call(bf16[512,2176]{1,0:T(8,128)(2,1)} %bitcast.36, bf16[704,2048]{1,0:T(8,128)(2,1)} %bitcast.49, bf16[704,2048]{1,0:T(8,128)(2,1)} %bitcast.53, bf16[704,2048]{1,0:T(8,128)(2,1)} %bitcast.57, ...), custom_call_target="tpu_custom_call" | custom-call | flops 4429185024 | bytes 17039360 | tf_op jit(solution)/shard_map/expert_forward/pallas_call | solution.py:171
  122.1 12.6 %expert_backward.2 = (bf16[512,2048]{1,0:T(8,128)(2,1)}, bf16[512,704]{1,0:T(8,128)(2,1)}, bf16[512,704]{1,0:T(8,128)(2,1)}, f32[512,128]{1,0:T(8,128)}) custom-call(bf16[512,2048]{1,0:T(8,128)(2,1)} %bitcast.15.gr_ref.x0_ref, f32[512,704]{1,0:T(8,128)} %get-tuple-element.31.g_ref, f32[512,704]{1,0:T(8,128)} %get-tuple-element.32.u_ref, ...), custom_call_target="tpu_custom_call" | custom-call | flops 4429185024 | bytes 17039360 | tf_op jit(solution)/shard_map/expert_backward/pallas_call | solution.py:210
  136.2 6.1 %join_back.1 = bf16[512,2432]{1,0:T(8,128)(2,1)} custom-call(bf16[512,2048]{1,0:T(8,128)(2,1)} %get-tuple-element.34.mine_ref, bf16[512,2048]{1,0:T(8,128)(2,1)} %copy-done.2, f32[512,128]{1,0:T(8,128)} %get-tuple-element.39.gg_ref, f32[512,128]{1,0:T(8,128)} %copy-done.4, f32[512,128]{1,0:T(8,128)} %get-tuple-element.33.gate_ref, ...), custom_call_target="tpu_custom_call" | custom-call | flops 10485760 | bytes 8388608 | tf_op jit(solution)/shard_map/join_back/pallas_call | solution.py:306
  142.3 6.2 %all-to-all-start.3 = ((bf16[64,8,2432]{2,1,0:T(8,128)(2,1)}), bf16[64,8,2432]{2,1,0:T(8,128)(2,1)S(1)}, u32[]{:S(2)}, u32[]{:S(2)}) async-start(bf16[64,8,2432]{2,1,0:T(8,128)(2,1)} %bitcast.40), calls=%async_computation.3 | async-start | bytes 4980736 | tf_op jit(solution)/shard_map/all_to_all | solution.py:435
  148.8 4.2 %collective-permute-done.1.sib_ref = bf16[512,2048]{1,0:T(8,128)(2,1)} collective-permute-done((bf16[512,2048]{1,0:T(8,128)(2,1)}, bf16[512,2048]{1,0:T(8,128)(2,1)}, u32[]{:S(2)}, u32[]{:S(2)}) %collective-permute-start.1) | collective-permute-done | bytes 2097184 | tf_op jit(solution)/shard_map/ppermute | solution.py:430
  153.1 4.3 %join_halves.1 = bf16[512,2048]{1,0:T(8,128)(2,1)} custom-call(bf16[512,2048]{1,0:T(8,128)(2,1)} %get-tuple-element.29.mine_ref, bf16[512,2048]{1,0:T(8,128)(2,1)} %collective-permute-done.1.sib_ref), custom_call_target="tpu_custom_call" | custom-call | flops 3145728 | bytes 6291456 | tf_op jit(solution)/shard_map/join_halves/pallas_call | solution.py:234
  157.4 23.2 %all-to-all-done.3 = bf16[64,8,2432]{2,1,0:T(8,128)(2,1)S(1)} async-done(((bf16[64,8,2432]{2,1,0:T(8,128)(2,1)}), bf16[64,8,2432]{2,1,0:T(8,128)(2,1)S(1)}, u32[]{:S(2)}, u32[]{:S(2)}) %all-to-all-start.3) | async-done | bytes 2490400 | tf_op jit(solution)/shard_map/all_to_all | solution.py:435
  182.1 9.3 %all-to-all-start.1 = ((bf16[64,8,2048]{2,1,0:T(8,128)(2,1)}), bf16[64,8,2048]{2,1,0:T(8,128)(2,1)}, u32[]{:S(2)}, u32[]{:S(2)}) async-start(bf16[64,8,2048]{2,1,0:T(8,128)(2,1)} %bitcast.41), calls=%async_computation.1 | async-start | bytes 4194304 | tf_op jit(solution)/shard_map/all_to_all | solution.py:435
  191.4 7.0 %shard_map.135 = bf16[704,2048]{1,0:T(8,128)(2,1)} custom-call(bf16[512,704]{1,0:T(8,128)(2,1)} %get-tuple-element.41.d0_ref, bf16[512,704]{1,0:T(8,128)(2,1)} %get-tuple-element.42.d1_ref, bf16[512,2176]{1,0:T(8,128)(2,1)} %bitcast.38, bf16[512,2176]{1,0:T(8,128)(2,1)} %collective-permute-done.x_ref.x1_ref), custom_call_target="tpu_custom_call" | custom-call | flops 2952790016 | bytes 7077888 | tf_op jit(solution)/shard_map/pallas_call | solution.py:254
  198.4 7.0 %shard_map.136 = bf16[704,2048]{1,0:T(8,128)(2,1)} custom-call(bf16[512,704]{1,0:T(8,128)(2,1)} %get-tuple-element.43.d0_ref, bf16[512,704]{1,0:T(8,128)(2,1)} %get-tuple-element.44.d1_ref, bf16[512,2176]{1,0:T(8,128)(2,1)} %bitcast.39, bf16[512,2176]{1,0:T(8,128)(2,1)} %collective-permute-done.x_ref.x1_ref), custom_call_target="tpu_custom_call" | custom-call | flops 2952790016 | bytes 7077888 | tf_op jit(solution)/shard_map/pallas_call | solution.py:254
  208.6 7.0 %shard_map.137 = bf16[704,2048]{1,0:T(8,128)(2,1)} custom-call(bf16[512,704]{1,0:T(8,128)(2,1)} %get-tuple-element.45.d0_ref, bf16[512,704]{1,0:T(8,128)(2,1)} %get-tuple-element.46.d1_ref, bf16[512,2048]{1,0:T(8,128)(2,1)} %bitcast.15.gr_ref.x0_ref, bf16[512,2048]{1,0:T(8,128)(2,1)} %collective-permute-done.2.gr_ref.x1_ref), custom_call_target="tpu_custom_call" | custom-call | flops 2952790016 | bytes 7077888 | tf_op jit(solution)/shard_map/pallas_call | solution.py:254
  215.6 3.0 %all-to-all-done.1 = bf16[64,8,2048]{2,1,0:T(8,128)(2,1)} async-done(((bf16[64,8,2048]{2,1,0:T(8,128)(2,1)}), bf16[64,8,2048]{2,1,0:T(8,128)(2,1)}, u32[]{:S(2)}, u32[]{:S(2)}) %all-to-all-start.1) | async-done | bytes 2097184 | tf_op jit(solution)/shard_map/all_to_all | solution.py:435
  218.6 4.5 %mix_outputs.1 = bf16[128,2048]{1,0:T(8,128)(2,1)} custom-call(bf16[512,128]{1,0:T(8,128)(2,1)} %get-tuple-element.27.place_ref, bf16[512,2048]{1,0:T(8,128)(2,1)} %bitcast.13.rows_ref, bf16[128,2048]{1,0:T(8,128)(2,1)} %tok_ref.5), custom_call_target="tpu_custom_call" | custom-call | flops 268435456 | bytes 2097152 | tf_op jit(solution)/shard_map/mix_outputs/pallas_call | solution.py:366
  223.1 5.1 %finish_tokens.1 = bf16[128,2048]{1,0:T(8,128)(2,1)} custom-call(bf16[512,128]{1,0:T(8,128)(2,1)} %get-tuple-element.27.place_ref, bf16[512,2432]{1,0:T(8,128)(2,1)} %bitcast.33, bf16[128,2048]{1,0:T(8,128)(2,1)} %tok_ref.5, f32[1,2048]{1,0:T(1,128)} %bitcast.45, bf16[128,2048]{1,0:T(8,128)(2,1)} %up_ref.1), custom_call_target="tpu_custom_call" | custom-call | flops 268435456 | bytes 2097152 | tf_op jit(solution)/shard_map/finish_tokens/pallas_call | solution.py:409
  (30 shorter events, 10.4 us)
Async XLA Ops:
  5.2 40.7 %all-to-all-start = ((bf16[64,8,2176]{2,1,0:T(8,128)(2,1)}), bf16[64,8,2176]{2,1,0:T(8,128)(2,1)S(1)}, u32[]{:S(2)}, u32[]{:S(2)}) async-start(bf16[64,8,2176]{2,1,0:T(8,128)(2,1)} %bitcast.43), calls=%async_computation | async-start | bytes 4456448 | tf_op jit(solution)/shard_map/all_to_all | solution.py:435
  45.9 7.8 %copy-start.1 = (bf16[64,8,2176]{2,1,0:T(8,128)(2,1)}, bf16[64,8,2176]{2,1,0:T(8,128)(2,1)S(1)}, u32[]{:S(2)}) copy-start(bf16[64,8,2176]{2,1,0:T(8,128)(2,1)S(1)} %all-to-all-done) | copy-start | bytes 6684676
  45.9 33.6 %all-to-all-start.2 = ((bf16[64,8,2048]{2,1,0:T(8,128)(2,1)}), bf16[64,8,2048]{2,1,0:T(8,128)(2,1)}, u32[]{:S(2)}, u32[]{:S(2)}) async-start(bf16[64,8,2048]{2,1,0:T(8,128)(2,1)} %bitcast.42), calls=%async_computation.2 | async-start | bytes 4194304 | tf_op jit(solution)/shard_map/all_to_all | solution.py:435
  53.7 31.9 %collective-permute-start = (bf16[512,2176]{1,0:T(8,128)(2,1)S(1)}, bf16[512,2176]{1,0:T(8,128)(2,1)}, u32[]{:S(2)}, u32[]{:S(2)}) collective-permute-start(bf16[512,2176]{1,0:T(8,128)(2,1)S(1)} %bitcast.34), channel_id=1, source_target_pairs={{0,1},{1,0},{2,3},{3,2},{4,5},{5,4},{6,7},{7,6},{8,9},{9,8},{10,11... | collective-permute-start | bytes 6684680 | tf_op jit(solution)/shard_map/ppermute | solution.py:430
  79.5 17.6 %collective-permute-start.2 = (bf16[512,2048]{1,0:T(8,128)(2,1)}, bf16[512,2048]{1,0:T(8,128)(2,1)}, u32[]{:S(2)}, u32[]{:S(2)}) collective-permute-start(bf16[512,2048]{1,0:T(8,128)(2,1)} %bitcast.15.gr_ref.x0_ref), channel_id=1, source_target_pairs={{0,1},{1,0},{2,3},{3,2},{4,5},{5,4},{6,7},{7,6},{8,9},{9,8},{10,11... | collective-permute-start | bytes 6291464 | tf_op jit(solution)/shard_map/ppermute | solution.py:430
  109.7 11.6 %copy-start.6 = (f32[512,128]{1,0:T(8,128)S(1)}, f32[512,128]{1,0:T(8,128)}, u32[]{:S(2)}) copy-start(f32[512,128]{1,0:T(8,128)} %get-tuple-element.40) | copy-start | bytes 786436
  109.7 25.0 %collective-permute-start.3 = (bf16[512,2048]{1,0:T(8,128)(2,1)}, bf16[512,2048]{1,0:T(8,128)(2,1)S(1)}, u32[]{:S(2)}, u32[]{:S(2)}) collective-permute-start(bf16[512,2048]{1,0:T(8,128)(2,1)} %get-tuple-element.38), channel_id=1, source_target_pairs={{0,1},{1,0},{2,3},{3,2},{4,5},{5,4},{6,7},{7,6},{8,9},{9,8},{10,11... | collective-permute-start | bytes 6291464 | tf_op jit(solution)/shard_map/ppermute | solution.py:430
  121.3 13.3 %collective-permute-start.4 = (f32[512,128]{1,0:T(8,128)S(1)}, f32[512,128]{1,0:T(8,128)S(1)}, u32[]{:S(2)}, u32[]{:S(2)}) collective-permute-start(f32[512,128]{1,0:T(8,128)S(1)} %copy-done.6), channel_id=1, source_target_pairs={{0,1},{1,0},{2,3},{3,2},{4,5},{5,4},{6,7},{7,6},{8,9},{9,8},{10,11... | collective-permute-start | bytes 786440 | tf_op jit(solution)/shard_map/ppermute | solution.py:430
  134.7 0.7 copy-start.4
  134.7 1.5 copy-start.2
  142.3 38.3 %all-to-all-start.3 = ((bf16[64,8,2432]{2,1,0:T(8,128)(2,1)}), bf16[64,8,2432]{2,1,0:T(8,128)(2,1)S(1)}, u32[]{:S(2)}, u32[]{:S(2)}) async-start(bf16[64,8,2432]{2,1,0:T(8,128)(2,1)} %bitcast.40), calls=%async_computation.3 | async-start | bytes 4980736 | tf_op jit(solution)/shard_map/all_to_all | solution.py:435
  148.5 4.6 %collective-permute-start.1 = (bf16[512,2048]{1,0:T(8,128)(2,1)}, bf16[512,2048]{1,0:T(8,128)(2,1)}, u32[]{:S(2)}, u32[]{:S(2)}) collective-permute-start(bf16[512,2048]{1,0:T(8,128)(2,1)} %get-tuple-element.30), channel_id=1, source_target_pairs={{0,1},{1,0},{2,3},{3,2},{4,5},{5,4},{6,7},{7,6},{8,9},{9,8},{10,11... | collective-permute-start | bytes 6291464 | tf_op jit(solution)/shard_map/ppermute | solution.py:430
  180.6 1.5 copy-start
  182.1 36.5 %all-to-all-start.1 = ((bf16[64,8,2048]{2,1,0:T(8,128)(2,1)}), bf16[64,8,2048]{2,1,0:T(8,128)(2,1)}, u32[]{:S(2)}, u32[]{:S(2)}) async-start(bf16[64,8,2048]{2,1,0:T(8,128)(2,1)} %bitcast.41), calls=%async_computation.1 | async-start | bytes 4194304 | tf_op jit(solution)/shard_map/all_to_all | solution.py:435
  207.2 20.9 %collective-permute-start.5 = (f32[72,256]{1,0:T(8,128)}, f32[72,256]{1,0:T(8,128)S(1)}, u32[]{:S(2)}, u32[]{:S(2)}) collective-permute-start(f32[72,256]{1,0:T(8,128)} %collect_sums.1), channel_id=1, source_target_pairs={{0,1},{1,0},{2,3},{3,2},{4,5},{5,4},{6,7},{7,6},{8,9},{9,8},{10,11... | collective-permute-start | bytes 221192 | tf_op jit(solution)/shard_map/ppermute | solution.py:430
  223.1 5.1 %copy-start.3 = (f32[72,256]{1,0:T(8,128)S(1)}, f32[72,256]{1,0:T(8,128)}, u32[]{:S(2)}) copy-start(f32[72,256]{1,0:T(8,128)} %collect_sums.1) | copy-start | bytes 221188
  223.1 5.8 %copy-start.5 = (f32[2048]{0:T(1024)S(1)}, f32[2048]{0:T(1024)}, u32[]{:S(2)}) copy-start(f32[2048]{0:T(1024)} %param.9) | copy-start | bytes 24580
where the time goes:
time: 232 us; the launch traced here: 229 us
  Pallas kernels  101 us (44%)
  waiting for transfers between devices  78.6 us (34%)
  starting transfers between devices  44.5 us (19%)
  local copies, waits for them, and re-layouts  3.61 us (2%)
    all_to_all x4, waiting for transfers between devices, exchange(): lax.all_to_all(x.reshape(experts, -1, width), CHIPS, 0, 0, tiled=True)  74.3 us
    all_to_all x4, starting transfers between devices, exchange(): lax.all_to_all(x.reshape(experts, -1, width), CHIPS, 0, 0, tiled=True)  35.2 us
    pallas_call x2, Pallas kernels, backward(): pl.pallas_call(backward_kernel, grid=(rows // blk,), out_shape=(jax.Shape...  25.3 us
    pallas_call x2, Pallas kernels, forward(): pl.pallas_call(forward_kernel, grid=(rows // blk,), out_shape=(jax.ShapeD...  23 us
    pallas_call x3, Pallas kernels, weight_grad(): pl.pallas_call(weight_grad_kernel, grid=(width // part,), out_shape=jax.S...  21 us
    ppermute x6, starting transfers between devices, across(): return lax.ppermute(block, axis, [(i, i ^ bit) for i in range(count)])  9.3 us
    pallas_call x1, Pallas kernels, join_back(): pl.pallas_call(join_kernel, grid=(chunks + 1,), out_shape=jax.ShapeDtypeS...  6.09 us
    pallas_call x1, Pallas kernels, finish(): pl.pallas_call(finish_kernel, grid=(slots // part,), out_shape=jax.ShapeD...  5.07 us
  transfers between devices with their start and end apart: 10, of which 5 were waited for; matrix products, arithmetic and copies ran while one was open for 0% of the time, Pallas kernels for 34%

commit v1 on v0

--- a/solution.py
+++ b/solution.py
@@ -16,6 +16,7 @@
 F32 = jnp.float32
 BF16 = jnp.bfloat16
 EPSILON = 1e-06
+KEEPING = 50 << 20
 
 
 def dot_nn(a, b):
@@ -28,6 +29,18 @@
 
 def dot_tn(a, b):
     return lax.dot_general(a, b, (((0,), (0,)), ((), ())), preferred_element_type=F32)
+
+
+VMEM = pl.BlockSpec(memory_space=pltpu.VMEM)
+HBM = pl.BlockSpec(memory_space=pltpu.HBM)
+
+
+def in_vmem(x):
+    return pltpu.with_memory_space_constraint(x, pltpu.VMEM)
+
+
+def in_hbm(x):
+    return pltpu.with_memory_space_constraint(x, pltpu.HBM)
 
 
 def cost(flops, bytes_accessed):
@@ -107,27 +120,6 @@
     )(tokens, gain, ids, router)
 
 
-def column_kernel(extra_ref, rc_ref):
-    extra = extra_ref[...].astype(F32)
-    rows_n, per_row = 8, 2
-    stride = extra.shape[0] // rows_n
-    parts = [extra[r * stride + j : r * stride + j + 1, :] for r in range(rows_n) for j in range(per_row)]
-    rc_ref[...] = jnp.broadcast_to(jnp.concatenate(parts, axis=1), rc_ref.shape).astype(BF16)
-
-
-def own_column(rows_in, width):
-    rows, _ = rows_in.shape
-    return pl.pallas_call(
-        column_kernel,
-        grid=(1,),
-        out_shape=jax.ShapeDtypeStruct((LANES, width), BF16),
-        in_specs=[pl.BlockSpec((rows, LANES), lambda i: (0, width // LANES))],
-        out_specs=whole((LANES, width)),
-        cost_estimate=cost(rows * LANES, 2 * LANES * (rows + width)),
-        name="own_column",
-    )(rows_in)
-
-
 def place_kernel(place_ref, x_ref, send_ref):
     send_ref[...] = dot_nn(place_ref[...], x_ref[...]).astype(BF16)
 
@@ -149,83 +141,169 @@
     )(place, x)
 
 
-def forward_kernel(x_ref, wg_ref, wu_ref, wd_ref, rc_ref, out_ref, hg_ref, g_ref, u_ref, gate_ref):
+def start_loads(sources, targets, sems):
+    @pl.when(pl.program_id(0) == 0)
+    def _():
+        for n, (source, target) in enumerate(zip(sources, targets)):
+            pltpu.make_async_copy(source, target, sems.at[n]).start()
+
+
+def wait_load(source, target, sems, n):
+    @pl.when(pl.program_id(0) == 0)
+    def _():
+        pltpu.make_async_copy(source, target, sems.at[n]).wait()
+
+
+def column_row(extra):
+    rows_n, per_row = 8, 2
+    stride = extra.shape[0] // rows_n
+    parts = [extra[r * stride + j : r * stride + j + 1, :] for r in range(rows_n) for j in range(per_row)]
+    return jnp.concatenate(parts, axis=1)
+
+
+def forward_body(x_ref, extra_ref, weights, sources, sems, outs, rc_scr):
+    wg_ref, wu_ref, wd_ref = weights
+    out_ref, hg_ref, g_ref, u_ref, gate_ref, rc_ref = outs
+    if sources:
+        start_loads(sources, weights, sems)
+
+    @pl.when(pl.program_id(0) == 0)
+    def _():
+        row = column_row(extra_ref[...].astype(F32))
+        rc_scr[...] = jnp.broadcast_to(row, rc_scr.shape).astype(BF16)
+        rc_ref[...] = jnp.broadcast_to(row, rc_ref.shape)
+
     x = x_ref[...]
-    gate = jax.nn.sigmoid(dot_nt(x, rc_ref[...]))
+    gate = jax.nn.sigmoid(dot_nt(x, rc_scr[...]))
+    gate_ref[...] = gate
+    if sources:
+        wait_load(sources[0], wg_ref, sems, 0)
     g = dot_nt(x, wg_ref[...])
+    g_ref[...] = g
+    if sources:
+        wait_load(sources[1], wu_ref, sems, 1)
     u = dot_nt(x, wu_ref[...])
-    hidden = g * jax.nn.sigmoid(g) * u
-    gated = (hidden * gate[:, :1]).astype(BF16)
+    u_ref[...] = u
+    gated = (g * jax.nn.sigmoid(g) * u * gate[:, :1]).astype(BF16)
+    hg_ref[...] = gated
+    if sources:
+        wait_load(sources[2], wd_ref, sems, 2)
     out_ref[...] = dot_nn(gated, wd_ref[...]).astype(BF16)
-    hg_ref[...] = gated
-    g_ref[...] = g
-    u_ref[...] = u
-    gate_ref[...] = gate
-
-
-def forward(x, wg, wu, wd, rc):
+
+
+def forward_loading_kernel(x_ref, extra_ref, sg, su, sd, *refs):
+    *outs, wg, wu, wd, rc_scr, sems = refs
+    forward_body(x_ref, extra_ref, (wg, wu, wd), (sg, su, sd), sems, outs, rc_scr)
+
+
+def forward_kernel(x_ref, extra_ref, wg, wu, wd, *refs):
+    *outs, rc_scr = refs
+    forward_body(x_ref, extra_ref, (wg, wu, wd), (), None, outs, rc_scr)
+
+
+def forward(x, weights, loading):
     rows = x.shape[0]
-    ff, width = wg.shape
+    ff, width = weights[0].shape
     blk = 256
     row_blk = lambda n: pl.BlockSpec((blk, n), lambda i: (i, 0))
-    return pl.pallas_call(
-        forward_kernel,
+    outs = [
+        jax.ShapeDtypeStruct((rows, width), BF16),
+        jax.ShapeDtypeStruct((rows, ff), BF16),
+        jax.ShapeDtypeStruct((rows, ff), F32),
+        jax.ShapeDtypeStruct((rows, ff), F32),
+        jax.ShapeDtypeStruct((rows, LANES), F32),
+        jax.ShapeDtypeStruct((CAP, width), F32),
+    ]
+    specs = [row_blk(width), row_blk(ff), row_blk(ff), row_blk(ff), row_blk(LANES), whole((CAP, width))]
+    scratch = [pltpu.VMEM((LANES, width), BF16)]
+    if loading:
+        outs += [pltpu.VMEM((ff, width), BF16)] * 3
+        specs += [VMEM] * 3
+        scratch += [pltpu.SemaphoreType.DMA((3,))]
+    got = pl.pallas_call(
+        forward_loading_kernel if loading else forward_kernel,
         grid=(rows // blk,),
-        out_shape=(
-            jax.ShapeDtypeStruct((rows, width), BF16),
-            jax.ShapeDtypeStruct((rows, ff), BF16),
-            jax.ShapeDtypeStruct((rows, ff), F32),
-            jax.ShapeDtypeStruct((rows, ff), F32),
-            jax.ShapeDtypeStruct((rows, LANES), F32),
-        ),
-        in_specs=[row_blk(width), whole((ff, width)), whole((ff, width)), whole((ff, width)), whole((LANES, width))],
-        out_specs=(row_blk(width), row_blk(ff), row_blk(ff), row_blk(ff), row_blk(LANES)),
-        compiler_params=pltpu.CompilerParams(dimension_semantics=("arbitrary",)),
+        out_shape=tuple(outs),
+        in_specs=[row_blk(width), pl.BlockSpec((rows, LANES), lambda i: (0, width // LANES))]
+        + [HBM if loading else VMEM] * 3,
+        out_specs=tuple(specs),
+        scratch_shapes=scratch,
+        compiler_params=pltpu.CompilerParams(dimension_semantics=("arbitrary",), vmem_limit_bytes=KEEPING),
         cost_estimate=cost(6 * rows * ff * width, 6 * ff * width + 8 * rows * width),
         name="expert_forward",
-    )(x, wg, wu, wd, rc)
-
-
-def backward_kernel(gr_ref, g_ref, u_ref, gate_ref, wg_ref, wu_ref, wd_ref, back_ref, dg_ref, du_ref, gg_ref):
+    )(x, x, *weights)
+    return got[:6], tuple(in_vmem(w) for w in got[6:])
+
+
+def backward_body(gr_ref, g_ref, u_ref, gate_ref, weights, sources, sems, outs):
+    wd_ref, wg_ref, wu_ref = weights
+    back_ref, dg_ref, du_ref, gg_ref = outs
+    if sources:
+        start_loads(sources, weights, sems)
+        wait_load(sources[0], wd_ref, sems, 0)
+    dh = dot_nt(gr_ref[...], wd_ref[...])
     g = g_ref[...]
     u = u_ref[...]
     s = jax.nn.sigmoid(g)
     act = g * s
-    dh = dot_nt(gr_ref[...], wd_ref[...])
-    inner = jnp.sum(dh * (act * u), axis=1, keepdims=True)
-    gg_ref[...] = jnp.broadcast_to(inner, gg_ref.shape)
+    gg_ref[...] = jnp.broadcast_to(jnp.sum(dh * (act * u), axis=1, keepdims=True), gg_ref.shape)
     dh = dh * gate_ref[:, :1]
     dg = (dh * u * s * (1.0 + g * (1.0 - s))).astype(BF16)
     du = (dh * act).astype(BF16)
     dg_ref[...] = dg
     du_ref[...] = du
-    back_ref[...] = (dot_nn(dg, wg_ref[...]) + dot_nn(du, wu_ref[...])).astype(BF16)
-
-
-def backward(gr, g, u, gate, wg, wu, wd):
+    if sources:
+        wait_load(sources[1], wg_ref, sems, 1)
+    back = dot_nn(dg, wg_ref[...])
+    if sources:
+        wait_load(sources[2], wu_ref, sems, 2)
+    back_ref[...] = (back + dot_nn(du, wu_ref[...])).astype(BF16)
+
+
+def backward_loading_kernel(gr, g, u, gate, sd, sg, su, *refs):
+    *outs, wd, wg, wu, sems = refs
+    backward_body(gr, g, u, gate, (wd, wg, wu), (sd, sg, su), sems, outs)
+
+
+def backward_kernel(gr, g, u, gate, wd, wg, wu, *outs):
+    backward_body(gr, g, u, gate, (wd, wg, wu), (), None, outs)
+
+
+def backward(gr, g, u, gate, weights, loading):
     rows, width = gr.shape
-    ff = wg.shape[0]
+    ff = weights[0].shape[0]
     blk = 256
     row_blk = lambda n: pl.BlockSpec((blk, n), lambda i: (i, 0))
-    return pl.pallas_call(
-        backward_kernel,
+    outs = [
+        jax.ShapeDtypeStruct((rows, width), BF16),
+        jax.ShapeDtypeStruct((rows, ff), BF16),
+        jax.ShapeDtypeStruct((rows, ff), BF16),
+        jax.ShapeDtypeStruct((rows, LANES), F32),
+    ]
+    specs = [row_blk(width), row_blk(ff), row_blk(ff), row_blk(LANES)]
+    scratch = []
+    if loading:
+        outs += [pltpu.VMEM((ff, width), BF16)] * 3
+        specs += [VMEM] * 3
+        scratch += [pltpu.SemaphoreType.DMA((3,))]
+    got = pl.pallas_call(
+        backward_loading_kernel if loading else backward_kernel,
         grid=(rows // blk,),
-        out_shape=(
-            jax.ShapeDtypeStruct((rows, width), BF16),
-            jax.ShapeDtypeStruct((rows, ff), BF16),
-            jax.ShapeDtypeStruct((rows, ff), BF16),
-            jax.ShapeDtypeStruct((rows, LANES), F32),
-        ),
-        in_specs=[row_blk(width), row_blk(ff), row_blk(ff), row_blk(LANES)] + [whole((ff, width))] * 3,
-        out_specs=(row_blk(width), row_blk(ff), row_blk(ff), row_blk(LANES)),
-        compiler_params=pltpu.CompilerParams(dimension_semantics=("arbitrary",)),
+        out_shape=tuple(outs),
+        in_specs=[row_blk(width), row_blk(ff), row_blk(ff), row_blk(LANES)] + [HBM if loading else VMEM] * 3,
+        out_specs=tuple(specs),
+        scratch_shapes=scratch,
+        compiler_params=pltpu.CompilerParams(dimension_semantics=("arbitrary",), vmem_limit_bytes=KEEPING),
         cost_estimate=cost(6 * rows * ff * width, 6 * ff * width + 8 * rows * width),
         name="expert_backward",
-    )(gr, g, u, gate, wg, wu, wd)
+    )(gr, g, u, gate, *weights)
+    return got[:4], tuple(in_vmem(w) for w in got[4:])
 
 
 def join_out_kernel(mine_ref, sib_ref, out_ref):
-    out_ref[...] = (mine_ref[...].astype(F32) + sib_ref[...].astype(F32)).astype(BF16)
+    rows = out_ref.shape[0]
+    sib = sib_ref[pl.ds(pl.multiple_of(pl.program_id(0) * rows, rows), rows), :]
+    out_ref[...] = (mine_ref[...].astype(F32) + sib.astype(F32)).astype(BF16)
 
 
 def join_halves(mine, sib):
@@ -235,12 +313,12 @@
         join_out_kernel,
         grid=(rows // 128,),
         out_shape=jax.ShapeDtypeStruct((rows, width), BF16),
-        in_specs=[blk, blk],
+        in_specs=[blk, VMEM],
         out_specs=blk,
-        compiler_params=pltpu.CompilerParams(dimension_semantics=("arbitrary",)),
+        compiler_params=pltpu.CompilerParams(dimension_semantics=("arbitrary",), vmem_limit_bytes=KEEPING),
         cost_estimate=cost(3 * rows * width, 6 * rows * width),
         name="join_halves",
-    )(mine, sib)
+    )(mine, in_vmem(sib))
 
 
 def weight_grad_kernel(d0_ref, d1_ref, x0_ref, x1_ref, out_ref):
@@ -273,7 +351,8 @@
         gate = gate_ref[...]
         gl = ((gg_ref[...] + gg_sib_ref[...]) * gate * (1.0 - gate)).astype(BF16).astype(F32)[:, :1]
         x = x_ref[...].astype(F32)
-        back = mine_ref[...].astype(F32) + sib_ref[...].astype(F32) + gl * rc_ref[:1, :].astype(F32)
+        sib = sib_ref[:, pl.ds(pl.multiple_of(c * part, part), part)]
+        back = mine_ref[...].astype(F32) + sib.astype(F32) + gl * rc_ref[:1, :]
         back_ref[...] = back.astype(BF16)
         gain_scr[c] = jnp.sum(x * back, axis=0, keepdims=True)
         router_scr[c] = jnp.sum(x * gl, axis=0, keepdims=True)
@@ -307,13 +386,13 @@
         join_kernel,
         grid=(chunks + 1,),
         out_shape=jax.ShapeDtypeStruct((rows, width + width // CAP + LANES), BF16),
-        in_specs=[col, col] + [whole((rows, LANES))] * 3 + [pl.BlockSpec((LANES, part), at), col],
+        in_specs=[col, VMEM] + [whole((rows, LANES))] * 3 + [pl.BlockSpec((CAP, part), at), col],
         out_specs=pl.BlockSpec((rows, part), lambda i: (0, i)),
         scratch_shapes=[pltpu.VMEM((chunks, 1, part), F32), pltpu.VMEM((chunks, 1, part), F32)],
-        compiler_params=pltpu.CompilerParams(dimension_semantics=("arbitrary",)),
+        compiler_params=pltpu.CompilerParams(dimension_semantics=("arbitrary",), vmem_limit_bytes=KEEPING),
         cost_estimate=cost(10 * rows * width, 8 * rows * width),
         name="join_back",
-    )(mine, sib, gg, gg_sib, gate, rc, x)
+    )(mine, in_vmem(sib), gg, gg_sib, gate, rc, x)
 
 
 def collect_kernel(a_ref, b_ref, c_ref, out_ref):
@@ -337,6 +416,7 @@
         out_shape=jax.ShapeDtypeStruct((CAP + rows // CAP, 2 * LANES), F32),
         in_specs=[lane(0), lane(1), lane(2)],
         out_specs=whole((CAP + rows // CAP, 2 * LANES)),
+        compiler_params=pltpu.CompilerParams(vmem_limit_bytes=KEEPING),
         cost_estimate=cost(rows * rows * LANES, 6 * rows * LANES),
         name="collect_sums",
     )(rows_in, rows_in, rows_in)
@@ -419,7 +499,7 @@
         ],
         out_specs=whole((tok_count, width)),
         scratch_shapes=[pltpu.VMEM((tok_count, width), F32)],
-        compiler_params=pltpu.CompilerParams(dimension_semantics=("arbitrary",)),
+        compiler_params=pltpu.CompilerParams(dimension_semantics=("arbitrary",), vmem_limit_bytes=KEEPING),
         cost_estimate=cost(2 * slots * tok_count * width, 2 * slots * width),
         name="finish_tokens",
     )(place, rows, tokens, gain, upstream)
@@ -443,22 +523,21 @@
     wg, wu, wd = w_gate[0].T, w_up[0].T, w_down[0]
 
     send_in, place = dispatch(tokens, gain, expert_ids.T, router_weight.T, slots)
-    in_0 = exchange(send_in, experts)
-    rc = own_column(in_0, width)
+    in_0 = in_hbm(exchange(send_in, experts))
     send_grad = place_rows(place, grad_mixed)
-    gr_0 = exchange(send_grad, experts)
+    gr_0 = in_hbm(exchange(send_grad, experts))
     in_1 = across(in_0, CORE, 1)
     gr_1 = across(gr_0, CORE, 1)
 
-    out_0, hg_0, g_0, u_0, gate_0 = forward(in_0, wg, wu, wd, rc)
-    out_1, hg_1, g_1, u_1, gate_1 = forward(in_1, wg, wu, wd, rc)
+    (out_1, hg_1, g_1, u_1, gate_1, _), near = forward(in_1, (wg, wu, wd), True)
+    (out_0, hg_0, g_0, u_0, gate_0, rc), _ = forward(in_0, near, False)
     out_s = across(out_1, CORE, 1)
     out = join_halves(out_0, out_s)
-    got_out = exchange(out, experts)
+    got_out = in_hbm(exchange(out, experts))
     mixed = mix(place, got_out, tokens)
 
-    back_0, dg_0, du_0, gg_0 = backward(gr_0, g_0, u_0, gate_0, wg, wu, wd)
-    back_1, dg_1, du_1, gg_1 = backward(gr_1, g_1, u_1, gate_1, wg, wu, wd)
+    (back_1, dg_1, du_1, gg_1), near = backward(gr_1, g_1, u_1, gate_1, (wd, wg, wu), True)
+    (back_0, dg_0, du_0, gg_0), _ = backward(gr_0, g_0, u_0, gate_0, near, False)
     back_s = across(back_1, CORE, 1)
     gg_s = across(gg_1, CORE, 1)
     back = join_back(back_0, back_s, gg_0, gg_s, gate_0, rc, in_0)

time: 232 us -> 238 us (1.026)
  local copies, waits for them, and re-layouts: 3.61 us -> 17.3 us
  Pallas kernels: 101 us -> 91.5 us
    unnamed x16 -> x36, local copies, waits for them, and re-layouts: 2.98 us -> 16.7 us
    pallas_call x5 -> x4, Pallas kernels: 50 us -> 44.3 us  [the longest x2 23.2 us: backward(): pl.pallas_call(backward_loading_kernel if loading else backward_kernel, g...]
  transfers between devices with their start and end apart: 10 -> 10, of which waited for: 5 -> 5; matrix products, arithmetic and copies ran while one was open for 0% -> 0% of each run, Pallas kernels for 34% -> 29%
where the time goes in v1:
time: 238 us; the launch traced here: 235 us
  Pallas kernels  91.5 us (38%)
  waiting for transfers between devices  79.9 us (34%)
  starting transfers between devices  44.1 us (19%)
  local copies, waits for them, and re-layouts  17.3 us (7%)
    all_to_all x4, waiting for transfers between devices, exchange(): lax.all_to_all(x.reshape(experts, -1, width), CHIPS, 0, 0, tiled=True)  75.8 us
    all_to_all x4, starting transfers between devices, exchange(): lax.all_to_all(x.reshape(experts, -1, width), CHIPS, 0, 0, tiled=True)  35.1 us
    pallas_call x2, Pallas kernels, backward(): pl.pallas_call(backward_loading_kernel if loading else backward_kernel, g...  23.2 us
    pallas_call x2, Pallas kernels, forward(): pl.pallas_call(forward_loading_kernel if loading else forward_kernel, gri...  21.1 us
    pallas_call x3, Pallas kernels, weight_grad(): pl.pallas_call(weight_grad_kernel, grid=(width // part,), out_shape=jax.S...  21 us
    unnamed x36, local copies, waits for them, and re-layouts  16.7 us
    ppermute x6, starting transfers between devices, across(): return lax.ppermute(block, axis, [(i, i ^ bit) for i in range(count)])  8.99 us
    pallas_call x1, Pallas kernels, join_back(): pl.pallas_call(join_kernel, grid=(chunks + 1,), out_shape=jax.ShapeDtypeS...  5.32 us
  transfers between devices with their start and end apart: 10, of which 5 were waited for; matrix products, arithmetic and copies ran while one was open for 0% of the time, Pallas kernels for 29%

profile of v1, /device:TPU:1, one launch (start us, length us, event | category | flops | bytes accessed | tf_op | source)
XLA Modules:
  0.0 235.2 jit_solution(14757501720096330248)
XLA Ops:
  0.6 4.6 %dispatch_tokens.1 = (bf16[512,2176]{1,0:T(8,128)(2,1)}, bf16[512,128]{1,0:T(8,128)(2,1)}) custom-call(bf16[128,2048]{1,0:T(8,128)(2,1)} %tok_ref.5, f32[1,2048]{1,0:T(1,128)} %bitcast.34, s32[3,128]{1,0:T(4,128)} %bitcast.54, bf16[64,256]{1,0:T(8,128)(2,1)} %bitcast.53), custom_call_target="tpu_custom_call" | custom-call | flops 268435456 | bytes 4194304 | tf_op jit(solution)/shard_map/dispatch_tokens/pallas_call | solution.py:104
  5.2 11.9 %all-to-all-start = ((bf16[64,8,2176]{2,1,0:T(8,128)(2,1)}), bf16[64,8,2176]{2,1,0:T(8,128)(2,1)S(1)}, u32[]{:S(2)}, u32[]{:S(2)}) async-start(bf16[64,8,2176]{2,1,0:T(8,128)(2,1)} %bitcast.45), calls=%async_computation | async-start | bytes 4456448 | tf_op jit(solution)/shard_map/all_to_all | solution.py:515
  17.2 4.0 %dispatch_grads.1 = bf16[512,2048]{1,0:T(8,128)(2,1)} custom-call(bf16[512,128]{1,0:T(8,128)(2,1)} %get-tuple-element.34.place_ref, bf16[128,2048]{1,0:T(8,128)(2,1)} %up_ref.1), custom_call_target="tpu_custom_call" | custom-call | flops 268435456 | bytes 4194304 | tf_op jit(solution)/shard_map/dispatch_grads/pallas_call | solution.py:132
  21.2 24.7 %all-to-all-done = bf16[64,8,2176]{2,1,0:T(8,128)(2,1)S(1)} async-done(((bf16[64,8,2176]{2,1,0:T(8,128)(2,1)}), bf16[64,8,2176]{2,1,0:T(8,128)(2,1)S(1)}, u32[]{:S(2)}, u32[]{:S(2)}) %all-to-all-start) | async-done | bytes 2228256 | tf_op jit(solution)/shard_map/all_to_all | solution.py:515
  45.9 7.8 %all-to-all-start.2 = ((bf16[64,8,2048]{2,1,0:T(8,128)(2,1)}), bf16[64,8,2048]{2,1,0:T(8,128)(2,1)}, u32[]{:S(2)}, u32[]{:S(2)}) async-start(bf16[64,8,2048]{2,1,0:T(8,128)(2,1)} %bitcast.44), calls=%async_computation.2 | async-start | bytes 4194304 | tf_op jit(solution)/shard_map/all_to_all | solution.py:515
  53.7 2.4 %collective-permute-start = (bf16[512,2176]{1,0:T(8,128)(2,1)S(1)}, bf16[512,2176]{1,0:T(8,128)(2,1)}, u32[]{:S(2)}, u32[]{:S(2)}) collective-permute-start(bf16[512,2176]{1,0:T(8,128)(2,1)S(1)} %bitcast.37), channel_id=1, source_target_pairs={{0,1},{1,0},{2,3},{3,2},{4,5},{5,4},{6,7},{7,6},{8,9},{9,8},{10,11... | collective-permute-start | bytes 6684680 | tf_op jit(solution)/shard_map/ppermute | solution.py:510
  56.1 23.4 %all-to-all-done.2 = bf16[64,8,2048]{2,1,0:T(8,128)(2,1)} async-done(((bf16[64,8,2048]{2,1,0:T(8,128)(2,1)}), bf16[64,8,2048]{2,1,0:T(8,128)(2,1)}, u32[]{:S(2)}, u32[]{:S(2)}) %all-to-all-start.2) | async-done | bytes 2097184 | tf_op jit(solution)/shard_map/all_to_all | solution.py:515
  79.5 4.3 %collective-permute-start.2 = (bf16[512,2048]{1,0:T(8,128)(2,1)}, bf16[512,2048]{1,0:T(8,128)(2,1)S(1)}, u32[]{:S(2)}, u32[]{:S(2)}) collective-permute-start(bf16[512,2048]{1,0:T(8,128)(2,1)} %bitcast.13.gr.x0_ref), channel_id=1, source_target_pairs={{0,1},{1,0},{2,3},{3,2},{4,5},{5,4},{6,7},{7,6},{8,9},{9,8},{10,11... | collective-permute-start | bytes 6291464 | tf_op jit(solution)/shard_map/ppermute | solution.py:510
  83.8 12.3 %expert_forward.2 = (bf16[512,2048]{1,0:T(8,128)(2,1)}, bf16[512,704]{1,0:T(8,128)(2,1)}, f32[512,704]{1,0:T(8,128)}, f32[512,704]{1,0:T(8,128)}, f32[512,128]{1...) custom-call(bf16[512,2176]{1,0:T(8,128)(2,1)} %collective-permute-do, ...), custom_call_target="tpu_custom_call" | custom-call | flops 4429185024 | bytes 17039360 | tf_op jit(solution)/shard_map/expert_forward/pallas_call | solution.py:223
  100.6 12.8 %expert_backward.2 = (bf16[512,2048]{1,0:T(8,128)(2,1)}, bf16[512,704]{1,0:T(8,128)(2,1)}, bf16[512,704]{1,0:T(8,128)(2,1)}, f32[512,128]{1,0:T(8,128)}, bf16[70...) custom-call(bf16[512,2048]{1,0:T(8,128)(2,1)} %copy-done.16, ...), custom_call_target="tpu_custom_call" | custom-call | flops 4429185024 | bytes 17039360 | tf_op jit(solution)/shard_map/expert_backward/pallas_call | solution.py:289
  120.7 8.7 %expert_forward.3 = (bf16[512,2048]{1,0:T(8,128)(2,1)}, bf16[512,704]{1,0:T(8,128)(2,1)}, f32[512,704]{1,0:T(8,128)}, f32[512,704]{1,0:T(8,128)}, f32[512,128]{1,0:T(8,128)}, /*index=5*/f32[8,2048]{1,0:T(8,128)}) custom-call(bf16[512,2176]{1,0:T(8,128)(2,1)} %bitcast.38, bf16[512,2176]{1,0:T(8,128)(2,1)} %bitcast.39, bf16[704,2048]{1,0:T(8,128)(2,1)S(1)} %copy-done.12, ...), custom_call_target="tpu_custom_call" | custom-call | flops 4429185024 | bytes 17039360 | tf_op jit(solution)/shard_map/expert_forward/pallas_call | solution.py:223
  133.1 10.4 %expert_backward.3 = (bf16[512,2048]{1,0:T(8,128)(2,1)}, bf16[512,704]{1,0:T(8,128)(2,1)}, bf16[512,704]{1,0:T(8,128)(2,1)}, f32[512,128]{1,0:T(8,128)}) custom-call(bf16[512,2048]{1,0:T(8,128)(2,1)} %bitcast.13.gr.x0_ref, f32[512,704]{1,0:T(8,128)} %get-tuple-element.41.g, f32[512,704]{1,0:T(8,128)} %get-tuple-element.42.u, ...), custom_call_target="tpu_custom_call" | custom-call | flops 4429185024 | bytes 17039360 | tf_op jit(solution)/shard_map/expert_backward/pallas_call | solution.py:289
  144.5 5.3 %join_back.1 = bf16[512,2432]{1,0:T(8,128)(2,1)} custom-call(bf16[512,2048]{1,0:T(8,128)(2,1)} %get-tuple-element.50.mine_ref, bf16[512,2048]{1,0:T(8,128)(2,1)S(1)} %collective-permute-done.3.sib_ref, f32[512,128]{1,0:T(8,128)S(1)} %copy-done.4, f32[512,128]{1,0:T(8,128)S(1)} %collective-permute-done.4.gg_sib_ref, f32[512,128]{1,0:T(8,128)S(1)} %copy-done.3, ...), custom_call_target="tpu_custom_call" | custom-call | flops 10485760 | bytes 8388608 | tf_op jit(solution)/shard_map/join_back/pallas_call | solution.py:385
  149.8 6.1 %all-to-all-start.3 = ((bf16[64,8,2432]{2,1,0:T(8,128)(2,1)}), bf16[64,8,2432]{2,1,0:T(8,128)(2,1)S(1)}, u32[]{:S(2)}, u32[]{:S(2)}) async-start(bf16[64,8,2432]{2,1,0:T(8,128)(2,1)} %bitcast.36), calls=%async_computation.3 | async-start | bytes 4980736 | tf_op jit(solution)/shard_map/all_to_all | solution.py:515
  156.3 4.1 %collective-permute-done.1.sib_ref = bf16[512,2048]{1,0:T(8,128)(2,1)S(1)} collective-permute-done((bf16[512,2048]{1,0:T(8,128)(2,1)}, bf16[512,2048]{1,0:T(8,128)(2,1)S(1)}, u32[]{:S(2)}, u32[]{:S(2)}) %collective-permute-start.1) | collective-permute-done | bytes 2097184 | tf_op jit(solution)/shard_map/ppermute | solution.py:510
  160.4 3.9 %join_halves.1 = bf16[512,2048]{1,0:T(8,128)(2,1)} custom-call(bf16[512,2048]{1,0:T(8,128)(2,1)} %get-tuple-element.39.mine_ref, bf16[512,2048]{1,0:T(8,128)(2,1)S(1)} %collective-permute-done.1.sib_ref), custom_call_target="tpu_custom_call" | custom-call | flops 3145728 | bytes 6291456 | tf_op jit(solution)/shard_map/join_halves/pallas_call | solution.py:312
  164.3 23.7 %all-to-all-done.3 = bf16[64,8,2432]{2,1,0:T(8,128)(2,1)S(1)} async-done(((bf16[64,8,2432]{2,1,0:T(8,128)(2,1)}), bf16[64,8,2432]{2,1,0:T(8,128)(2,1)S(1)}, u32[]{:S(2)}, u32[]{:S(2)}) %all-to-all-start.3) | async-done | bytes 2490400 | tf_op jit(solution)/shard_map/all_to_all | solution.py:515
  188.1 9.2 %all-to-all-start.1 = ((bf16[64,8,2048]{2,1,0:T(8,128)(2,1)}), bf16[64,8,2048]{2,1,0:T(8,128)(2,1)}, u32[]{:S(2)}, u32[]{:S(2)}) async-start(bf16[64,8,2048]{2,1,0:T(8,128)(2,1)} %bitcast.43), calls=%async_computation.1 | async-start | bytes 4194304 | tf_op jit(solution)/shard_map/all_to_all | solution.py:515
  197.3 7.0 %shard_map.135 = bf16[704,2048]{1,0:T(8,128)(2,1)} custom-call(bf16[512,704]{1,0:T(8,128)(2,1)} %get-tuple-element.55.d0_ref, bf16[512,704]{1,0:T(8,128)(2,1)} %get-tuple-element.56.d1_ref, bf16[512,2176]{1,0:T(8,128)(2,1)} %bitcast.41, bf16[512,2176]{1,0:T(8,128)(2,1)} %collective-permute-done.x_ref.extra_ref.x1_ref), custom_call_target="tpu_custom_call" | custom-call | flops 2952790016 | bytes 7077888 | tf_op jit(solution)/shard_map/pallas_call | solution.py:332
  204.3 7.0 %shard_map.136 = bf16[704,2048]{1,0:T(8,128)(2,1)} custom-call(bf16[512,704]{1,0:T(8,128)(2,1)} %get-tuple-element.57.d0_ref, bf16[512,704]{1,0:T(8,128)(2,1)} %get-tuple-element.58.d1_ref, bf16[512,2176]{1,0:T(8,128)(2,1)} %bitcast.42, bf16[512,2176]{1,0:T(8,128)(2,1)} %collective-permute-done.x_ref.extra_ref.x1_ref), custom_call_target="tpu_custom_call" | custom-call | flops 2952790016 | bytes 7077888 | tf_op jit(solution)/shard_map/pallas_call | solution.py:332
  213.5 7.0 %shard_map.137 = bf16[704,2048]{1,0:T(8,128)(2,1)} custom-call(bf16[512,704]{1,0:T(8,128)(2,1)} %get-tuple-element.59.d0_ref, bf16[512,704]{1,0:T(8,128)(2,1)} %get-tuple-element.60.d1_ref, bf16[512,2048]{1,0:T(8,128)(2,1)} %bitcast.13.gr.x0_ref, bf16[512,2048]{1,0:T(8,128)(2,1)} %copy-done.16), custom_call_target="tpu_custom_call" | custom-call | flops 2952790016 | bytes 7077888 | tf_op jit(solution)/shard_map/pallas_call | solution.py:332
  220.5 4.0 %all-to-all-done.1 = bf16[64,8,2048]{2,1,0:T(8,128)(2,1)} async-done(((bf16[64,8,2048]{2,1,0:T(8,128)(2,1)}), bf16[64,8,2048]{2,1,0:T(8,128)(2,1)}, u32[]{:S(2)}, u32[]{:S(2)}) %all-to-all-start.1) | async-done | bytes 2097184 | tf_op jit(solution)/shard_map/all_to_all | solution.py:515
  224.5 4.5 %mix_outputs.1 = bf16[128,2048]{1,0:T(8,128)(2,1)} custom-call(bf16[512,128]{1,0:T(8,128)(2,1)} %get-tuple-element.34.place_ref, bf16[512,2048]{1,0:T(8,128)(2,1)} %bitcast.11.rows_ref, bf16[128,2048]{1,0:T(8,128)(2,1)} %tok_ref.5), custom_call_target="tpu_custom_call" | custom-call | flops 268435456 | bytes 2097152 | tf_op jit(solution)/shard_map/mix_outputs/pallas_call | solution.py:446
  229.9 3.1 %finish_tokens.1 = bf16[128,2048]{1,0:T(8,128)(2,1)} custom-call(bf16[512,128]{1,0:T(8,128)(2,1)S(1)} %copy-done.2, bf16[512,2432]{1,0:T(8,128)(2,1)S(1)} %bitcast.33, bf16[128,2048]{1,0:T(8,128)(2,1)S(1)} %copy-done, f32[1,2048]{1,0:T(1,128)S(1)} %bitcast.35, bf16[128,2048]{1,0:T(8,128)(2,1)S(1)} %copy-done.1), custom_call_target="tpu_custom_call" | custom-call | flops 268435456 | bytes 2097152 | tf_op jit(solution)/shard_map/finish_tokens/pallas_call | solution.py:489
  (49 shorter events, 22.0 us)
Async XLA Ops:
  5.2 40.7 %all-to-all-start = ((bf16[64,8,2176]{2,1,0:T(8,128)(2,1)}), bf16[64,8,2176]{2,1,0:T(8,128)(2,1)S(1)}, u32[]{:S(2)}, u32[]{:S(2)}) async-start(bf16[64,8,2176]{2,1,0:T(8,128)(2,1)} %bitcast.45), calls=%async_computation | async-start | bytes 4456448 | tf_op jit(solution)/shard_map/all_to_all | solution.py:515
  45.9 50.3 %copy-start.15 = (bf16[64,8,2176]{2,1,0:T(8,128)(2,1)}, bf16[64,8,2176]{2,1,0:T(8,128)(2,1)S(1)}, u32[]{:S(2)}) copy-start(bf16[64,8,2176]{2,1,0:T(8,128)(2,1)S(1)} %all-to-all-done) | copy-start | bytes 6684676
  45.9 33.6 %all-to-all-start.2 = ((bf16[64,8,2048]{2,1,0:T(8,128)(2,1)}), bf16[64,8,2048]{2,1,0:T(8,128)(2,1)}, u32[]{:S(2)}, u32[]{:S(2)}) async-start(bf16[64,8,2048]{2,1,0:T(8,128)(2,1)} %bitcast.44), calls=%async_computation.2 | async-start | bytes 4194304 | tf_op jit(solution)/shard_map/all_to_all | solution.py:515
  53.7 30.1 %collective-permute-start = (bf16[512,2176]{1,0:T(8,128)(2,1)S(1)}, bf16[512,2176]{1,0:T(8,128)(2,1)}, u32[]{:S(2)}, u32[]{:S(2)}) collective-permute-start(bf16[512,2176]{1,0:T(8,128)(2,1)S(1)} %bitcast.37), channel_id=1, source_target_pairs={{0,1},{1,0},{2,3},{3,2},{4,5},{5,4},{6,7},{7,6},{8,9},{9,8},{10,11... | collective-permute-start | bytes 6684680 | tf_op jit(solution)/shard_map/ppermute | solution.py:510
  79.5 19.8 %collective-permute-start.2 = (bf16[512,2048]{1,0:T(8,128)(2,1)}, bf16[512,2048]{1,0:T(8,128)(2,1)S(1)}, u32[]{:S(2)}, u32[]{:S(2)}) collective-permute-start(bf16[512,2048]{1,0:T(8,128)(2,1)} %bitcast.13.gr.x0_ref), channel_id=1, source_target_pairs={{0,1},{1,0},{2,3},{3,2},{4,5},{5,4},{6,7},{7,6},{8,9},{9,8},{10,11... | collective-permute-start | bytes 6291464 | tf_op jit(solution)/shard_map/ppermute | solution.py:510
  96.2 1.6 copy-start.11
  97.7 1.6 copy-start.13
  113.4 1.6 copy-start.7
  115.0 1.6 copy-start.9
  116.6 27.0 %collective-permute-start.3 = (bf16[512,2048]{1,0:T(8,128)(2,1)}, bf16[512,2048]{1,0:T(8,128)(2,1)S(1)}, u32[]{:S(2)}, u32[]{:S(2)}) collective-permute-start(bf16[512,2048]{1,0:T(8,128)(2,1)} %get-tuple-element.51), channel_id=1, source_target_pairs={{0,1},{1,0},{2,3},{3,2},{4,5},{5,4},{6,7},{7,6},{8,9},{9,8},{10,11... | collective-permute-start | bytes 6291464 | tf_op jit(solution)/shard_map/ppermute | solution.py:510
  116.6 26.9 %collective-permute-start.4 = (f32[512,128]{1,0:T(8,128)}, f32[512,128]{1,0:T(8,128)S(1)}, u32[]{:S(2)}, u32[]{:S(2)}) collective-permute-start(f32[512,128]{1,0:T(8,128)} %get-tuple-element.53), channel_id=1, source_target_pairs={{0,1},{1,0},{2,3},{3,2},{4,5},{5,4},{6,7},{7,6},{8,9},{9,8},{10,11... | collective-permute-start | bytes 786440 | tf_op jit(solution)/shard_map/ppermute | solution.py:510
  117.1 1.8 copy-start.12
  118.9 1.8 copy-start.14
  129.5 1.8 copy-start.8
  131.3 1.8 copy-start.10
  133.1 10.4 %copy-start.3 = (f32[512,128]{1,0:T(8,128)S(1)}, f32[512,128]{1,0:T(8,128)}, u32[]{:S(2)}) copy-start(f32[512,128]{1,0:T(8,128)} %get-tuple-element.43.gate.gate_ref) | copy-start | bytes 786436
  133.1 10.5 %copy-start.5 = (f32[8,2048]{1,0:T(8,128)S(1)}, f32[8,2048]{1,0:T(8,128)}, u32[]{:S(2)}) copy-start(f32[8,2048]{1,0:T(8,128)} %get-tuple-element.54.rc_ref) | copy-start | bytes 196612
  149.8 38.2 %all-to-all-start.3 = ((bf16[64,8,2432]{2,1,0:T(8,128)(2,1)}), bf16[64,8,2432]{2,1,0:T(8,128)(2,1)S(1)}, u32[]{:S(2)}, u32[]{:S(2)}) async-start(bf16[64,8,2432]{2,1,0:T(8,128)(2,1)} %bitcast.36), calls=%async_computation.3 | async-start | bytes 4980736 | tf_op jit(solution)/shard_map/all_to_all | solution.py:515
  155.9 4.5 %collective-permute-start.1 = (bf16[512,2048]{1,0:T(8,128)(2,1)}, bf16[512,2048]{1,0:T(8,128)(2,1)S(1)}, u32[]{:S(2)}, u32[]{:S(2)}) collective-permute-start(bf16[512,2048]{1,0:T(8,128)(2,1)} %get-tuple-element.40), channel_id=1, source_target_pairs={{0,1},{1,0},{2,3},{3,2},{4,5},{5,4},{6,7},{7,6},{8,9},{9,8},{10,11... | collective-permute-start | bytes 6291464 | tf_op jit(solution)/shard_map/ppermute | solution.py:510
  188.1 36.4 %all-to-all-start.1 = ((bf16[64,8,2048]{2,1,0:T(8,128)(2,1)}), bf16[64,8,2048]{2,1,0:T(8,128)(2,1)}, u32[]{:S(2)}, u32[]{:S(2)}) async-start(bf16[64,8,2048]{2,1,0:T(8,128)(2,1)} %bitcast.43), calls=%async_computation.1 | async-start | bytes 4194304 | tf_op jit(solution)/shard_map/all_to_all | solution.py:515
  212.2 20.8 %collective-permute-start.5 = (f32[72,256]{1,0:T(8,128)}, f32[72,256]{1,0:T(8,128)}, u32[]{:S(2)}, u32[]{:S(2)}) collective-permute-start(f32[72,256]{1,0:T(8,128)} %collect_sums.1), channel_id=1, source_target_pairs={{0,1},{1,0},{2,3},{3,2},{4,5},{5,4},{6,7},{7,6},{8,9},{9,8},{10,11... | collective-permute-start | bytes 221192 | tf_op jit(solution)/shard_map/ppermute | solution.py:510
  220.5 8.5 %copy-start = (bf16[128,2048]{1,0:T(8,128)(2,1)S(1)}, bf16[128,2048]{1,0:T(8,128)(2,1)}, u32[]{:S(2)}) copy-start(bf16[128,2048]{1,0:T(8,128)(2,1)} %tok_ref.5) | copy-start | bytes 1572868
  220.5 8.5 %copy-start.1 = (bf16[128,2048]{1,0:T(8,128)(2,1)S(1)}, bf16[128,2048]{1,0:T(8,128)(2,1)}, u32[]{:S(2)}) copy-start(bf16[128,2048]{1,0:T(8,128)(2,1)} %up_ref.1) | copy-start | bytes 1572868
  220.5 8.5 %copy-start.6 = (f32[2048]{0:T(1024)S(1)}, f32[2048]{0:T(1024)}, u32[]{:S(2)}) copy-start(f32[2048]{0:T(1024)} %param.9) | copy-start | bytes 24580
  (3 other events, 3.2 us)

commit v2 on v1

--- a/solution.py
+++ b/solution.py
@@ -16,7 +16,7 @@
 F32 = jnp.float32
 BF16 = jnp.bfloat16
 EPSILON = 1e-06
-KEEPING = 50 << 20
+KEEPING = 51 << 20
 
 
 def dot_nn(a, b):
@@ -141,17 +141,19 @@
     )(place, x)
 
 
-def start_loads(sources, targets, sems):
-    @pl.when(pl.program_id(0) == 0)
-    def _():
-        for n, (source, target) in enumerate(zip(sources, targets)):
-            pltpu.make_async_copy(source, target, sems.at[n]).start()
-
-
-def wait_load(source, target, sems, n):
-    @pl.when(pl.program_id(0) == 0)
-    def _():
-        pltpu.make_async_copy(source, target, sems.at[n]).wait()
+CHUNKS = 4
+
+
+class Copies:
+    def __init__(self, sems):
+        self.sems = sems
+        self.started = []
+
+    def start(self, source, target):
+        copy = pltpu.make_async_copy(source, target, self.sems.at[len(self.started)])
+        copy.start()
+        self.started.append(copy)
+        return copy
 
 
 def column_row(extra):
@@ -161,149 +163,164 @@
     return jnp.concatenate(parts, axis=1)
 
 
-def forward_body(x_ref, extra_ref, weights, sources, sems, outs, rc_scr):
-    wg_ref, wu_ref, wd_ref = weights
-    out_ref, hg_ref, g_ref, u_ref, gate_ref, rc_ref = outs
-    if sources:
-        start_loads(sources, weights, sems)
-
-    @pl.when(pl.program_id(0) == 0)
-    def _():
-        row = column_row(extra_ref[...].astype(F32))
-        rc_scr[...] = jnp.broadcast_to(row, rc_scr.shape).astype(BF16)
-        rc_ref[...] = jnp.broadcast_to(row, rc_ref.shape)
-
-    x = x_ref[...]
-    gate = jax.nn.sigmoid(dot_nt(x, rc_scr[...]))
+def forward_body(x_hbm, weights, sources, outs, scratch):
+    wg, wu, wd = weights
+    out_hbm, hg_hbm, fg_hbm, fu_hbm, gate_ref, rc_ref = outs
+    block, hg, fg, fu, sems = scratch
+    width = wd.shape[1]
+    copies = Copies(sems)
+    x, out = (x_hbm, block) if sources else (block, out_hbm)
+    if not sources:
+        copies.start(x_hbm, x).wait()
+    got_w = [copies.start(source, target) for source, target in zip(sources, weights)]
+    waits = lambda n: got_w[n].wait() if got_w else None
+    rows = x[:, :width]
+    row = column_row(x[:, width:].astype(F32))
+    rc_ref[...] = jnp.broadcast_to(row, rc_ref.shape)
+    gate = jax.nn.sigmoid(dot_nt(rows, jnp.broadcast_to(row, (LANES, width)).astype(BF16)))
     gate_ref[...] = gate
-    if sources:
-        wait_load(sources[0], wg_ref, sems, 0)
-    g = dot_nt(x, wg_ref[...])
-    g_ref[...] = g
-    if sources:
-        wait_load(sources[1], wu_ref, sems, 1)
-    u = dot_nt(x, wu_ref[...])
-    u_ref[...] = u
-    gated = (g * jax.nn.sigmoid(g) * u * gate[:, :1]).astype(BF16)
-    hg_ref[...] = gated
-    if sources:
-        wait_load(sources[2], wd_ref, sems, 2)
-    out_ref[...] = dot_nn(gated, wd_ref[...]).astype(BF16)
-
-
-def forward_loading_kernel(x_ref, extra_ref, sg, su, sd, *refs):
-    *outs, wg, wu, wd, rc_scr, sems = refs
-    forward_body(x_ref, extra_ref, (wg, wu, wd), (sg, su, sd), sems, outs, rc_scr)
-
-
-def forward_kernel(x_ref, extra_ref, wg, wu, wd, *refs):
-    *outs, rc_scr = refs
-    forward_body(x_ref, extra_ref, (wg, wu, wd), (), None, outs, rc_scr)
+    gate = gate[:, :1]
+    waits(0)
+    g = dot_nt(rows, wg[...])
+    waits(1)
+    u = dot_nt(rows, wu[...])
+    s = jax.nn.sigmoid(g)
+    act = gate * (g * s)
+    hg[...] = (act * u).astype(BF16)
+    fu[...] = act.astype(BF16)
+    fg[...] = (gate * s * u * (1.0 + g * (1.0 - s))).astype(BF16)
+    puts = [copies.start(hg, hg_hbm), copies.start(fg, fg_hbm), copies.start(fu, fu_hbm)]
+    waits(2)
+    part = width // CHUNKS
+    for c in range(CHUNKS):
+        cols = slice(c * part, (c + 1) * part)
+        out[:, cols] = dot_nn(hg[...], wd[:, cols]).astype(BF16)
+        if sources:
+            puts.append(copies.start(out.at[:, cols], out_hbm.at[:, cols]))
+    for put in puts:
+        put.wait()
+
+
+def forward_loading_kernel(x_hbm, sg, su, sd, *refs):
+    forward_body(x_hbm, refs[6:9], (sg, su, sd), refs[:6], refs[9:])
+
+
+def forward_kernel(x_hbm, wg, wu, wd, *refs):
+    forward_body(x_hbm, (wg, wu, wd), (), refs[:6], refs[6:])
 
 
 def forward(x, weights, loading):
     rows = x.shape[0]
     ff, width = weights[0].shape
-    blk = 256
-    row_blk = lambda n: pl.BlockSpec((blk, n), lambda i: (i, 0))
     outs = [
-        jax.ShapeDtypeStruct((rows, width), BF16),
+        jax.ShapeDtypeStruct((rows, width), BF16) if loading else pltpu.VMEM((rows, width), BF16),
         jax.ShapeDtypeStruct((rows, ff), BF16),
-        jax.ShapeDtypeStruct((rows, ff), F32),
-        jax.ShapeDtypeStruct((rows, ff), F32),
+        jax.ShapeDtypeStruct((rows, ff), BF16),
+        jax.ShapeDtypeStruct((rows, ff), BF16),
         jax.ShapeDtypeStruct((rows, LANES), F32),
         jax.ShapeDtypeStruct((CAP, width), F32),
     ]
-    specs = [row_blk(width), row_blk(ff), row_blk(ff), row_blk(ff), row_blk(LANES), whole((CAP, width))]
-    scratch = [pltpu.VMEM((LANES, width), BF16)]
+    specs = [HBM if loading else VMEM] + [HBM] * 3 + [whole((rows, LANES)), whole((CAP, width))]
     if loading:
         outs += [pltpu.VMEM((ff, width), BF16)] * 3
         specs += [VMEM] * 3
-        scratch += [pltpu.SemaphoreType.DMA((3,))]
     got = pl.pallas_call(
         forward_loading_kernel if loading else forward_kernel,
-        grid=(rows // blk,),
+        grid=(1,),
         out_shape=tuple(outs),
-        in_specs=[row_blk(width), pl.BlockSpec((rows, LANES), lambda i: (0, width // LANES))]
-        + [HBM if loading else VMEM] * 3,
+        in_specs=[VMEM if loading else HBM] + [HBM if loading else VMEM] * 3,
         out_specs=tuple(specs),
-        scratch_shapes=scratch,
+        scratch_shapes=[
+            pltpu.VMEM((rows, width) if loading else x.shape, BF16),
+            pltpu.VMEM((rows, ff), BF16),
+            pltpu.VMEM((rows, ff), BF16),
+            pltpu.VMEM((rows, ff), BF16),
+            pltpu.SemaphoreType.DMA((7 + CHUNKS,)),
+        ],
         compiler_params=pltpu.CompilerParams(dimension_semantics=("arbitrary",), vmem_limit_bytes=KEEPING),
         cost_estimate=cost(6 * rows * ff * width, 6 * ff * width + 8 * rows * width),
         name="expert_forward",
-    )(x, x, *weights)
+    )(in_vmem(x) if loading else x, *weights)
     return got[:6], tuple(in_vmem(w) for w in got[6:])
 
 
-def backward_body(gr_ref, g_ref, u_ref, gate_ref, weights, sources, sems, outs):
-    wd_ref, wg_ref, wu_ref = weights
-    back_ref, dg_ref, du_ref, gg_ref = outs
-    if sources:
-        start_loads(sources, weights, sems)
-        wait_load(sources[0], wd_ref, sems, 0)
-    dh = dot_nt(gr_ref[...], wd_ref[...])
-    g = g_ref[...]
-    u = u_ref[...]
-    s = jax.nn.sigmoid(g)
-    act = g * s
-    gg_ref[...] = jnp.broadcast_to(jnp.sum(dh * (act * u), axis=1, keepdims=True), gg_ref.shape)
-    dh = dh * gate_ref[:, :1]
-    dg = (dh * u * s * (1.0 + g * (1.0 - s))).astype(BF16)
-    du = (dh * act).astype(BF16)
-    dg_ref[...] = dg
-    du_ref[...] = du
-    if sources:
-        wait_load(sources[1], wg_ref, sems, 1)
-    back = dot_nn(dg, wg_ref[...])
-    if sources:
-        wait_load(sources[2], wu_ref, sems, 2)
-    back_ref[...] = (back + dot_nn(du, wu_ref[...])).astype(BF16)
-
-
-def backward_loading_kernel(gr, g, u, gate, sd, sg, su, *refs):
-    *outs, wd, wg, wu, sems = refs
-    backward_body(gr, g, u, gate, (wd, wg, wu), (sd, sg, su), sems, outs)
-
-
-def backward_kernel(gr, g, u, gate, wd, wg, wu, *outs):
-    backward_body(gr, g, u, gate, (wd, wg, wu), (), None, outs)
-
-
-def backward(gr, g, u, gate, weights, loading):
+def backward_body(ins, weights, sources, outs, scratch):
+    wd, wg, wu = weights
+    back_hbm, dg_hbm, du_hbm, gg_ref = outs
+    block, hg, fg, fu, dg, du, sems = scratch
+    width = wd.shape[1]
+    copies = Copies(sems)
+    gr, back = (ins[0], block) if sources else (block, back_hbm)
+    got = [] if sources else [copies.start(ins[0], gr)]
+    got_w = [copies.start(source, target) for source, target in zip(sources[:1], weights[:1])]
+    got_more = [copies.start(source, target) for source, target in zip(ins[1:], (hg, fg, fu))]
+    got_w += [copies.start(source, target) for source, target in zip(sources[1:], weights[1:])]
+    waits = lambda n: got_w[n].wait() if got_w else None
+    for copy in got:
+        copy.wait()
+    waits(0)
+    dh = dot_nt(gr[...], wd[...])
+    for copy in got_more:
+        copy.wait()
+    inner = jnp.sum(dh * hg[...].astype(F32), axis=1, keepdims=True)
+    gg_ref[...] = jnp.broadcast_to(inner, gg_ref.shape)
+    dg[...] = (dh * fg[...].astype(F32)).astype(BF16)
+    du[...] = (dh * fu[...].astype(F32)).astype(BF16)
+    puts = [copies.start(dg, dg_hbm), copies.start(du, du_hbm)]
+    waits(1)
+    waits(2)
+    part = width // CHUNKS
+    for c in range(CHUNKS):
+        cols = slice(c * part, (c + 1) * part)
+        back[:, cols] = (dot_nn(dg[...], wg[:, cols]) + dot_nn(du[...], wu[:, cols])).astype(BF16)
+        if sources:
+            puts.append(copies.start(back.at[:, cols], back_hbm.at[:, cols]))
+    for put in puts:
+        put.wait()
+
+
+def backward_loading_kernel(gr, hg, fg, fu, sd, sg, su, *refs):
+    backward_body((gr, hg, fg, fu), refs[4:7], (sd, sg, su), refs[:4], refs[7:])
+
+
+def backward_kernel(gr, hg, fg, fu, wd, wg, wu, *refs):
+    backward_body((gr, hg, fg, fu), (wd, wg, wu), (), refs[:4], refs[4:])
+
+
+def backward(gr, hg, fg, fu, weights, loading):
     rows, width = gr.shape
     ff = weights[0].shape[0]
-    blk = 256
-    row_blk = lambda n: pl.BlockSpec((blk, n), lambda i: (i, 0))
     outs = [
-        jax.ShapeDtypeStruct((rows, width), BF16),
+        jax.ShapeDtypeStruct((rows, width), BF16) if loading else pltpu.VMEM((rows, width), BF16),
         jax.ShapeDtypeStruct((rows, ff), BF16),
         jax.ShapeDtypeStruct((rows, ff), BF16),
         jax.ShapeDtypeStruct((rows, LANES), F32),
     ]
-    specs = [row_blk(width), row_blk(ff), row_blk(ff), row_blk(LANES)]
-    scratch = []
+    specs = [HBM if loading else VMEM] + [HBM] * 2 + [whole((rows, LANES))]
     if loading:
         outs += [pltpu.VMEM((ff, width), BF16)] * 3
         specs += [VMEM] * 3
-        scratch += [pltpu.SemaphoreType.DMA((3,))]
     got = pl.pallas_call(
         backward_loading_kernel if loading else backward_kernel,
-        grid=(rows // blk,),
+        grid=(1,),
         out_shape=tuple(outs),
-        in_specs=[row_blk(width), row_blk(ff), row_blk(ff), row_blk(LANES)] + [HBM if loading else VMEM] * 3,
+        in_specs=[VMEM if loading else HBM] + [HBM] * 3 + [HBM if loading else VMEM] * 3,
         out_specs=tuple(specs),
-        scratch_shapes=scratch,
+        scratch_shapes=[pltpu.VMEM((rows, width), BF16)]
+        + [pltpu.VMEM((rows, ff), BF16)] * 3
+        + [pltpu.VMEM((rows, ff), BF16)] * 2
+        + [pltpu.SemaphoreType.DMA((9 + CHUNKS,))],
         compiler_params=pltpu.CompilerParams(dimension_semantics=("arbitrary",), vmem_limit_bytes=KEEPING),
         cost_estimate=cost(6 * rows * ff * width, 6 * ff * width + 8 * rows * width),
         name="expert_backward",
-    )(gr, g, u, gate, *weights)
+    )(in_vmem(gr) if loading else gr, hg, fg, fu, *weights)
     return got[:4], tuple(in_vmem(w) for w in got[4:])
 
 
 def join_out_kernel(mine_ref, sib_ref, out_ref):
     rows = out_ref.shape[0]
-    sib = sib_ref[pl.ds(pl.multiple_of(pl.program_id(0) * rows, rows), rows), :]
-    out_ref[...] = (mine_ref[...].astype(F32) + sib.astype(F32)).astype(BF16)
+    here = pl.ds(pl.multiple_of(pl.program_id(0) * rows, rows), rows)
+    out_ref[...] = (mine_ref[here, :].astype(F32) + sib_ref[here, :].astype(F32)).astype(BF16)
 
 
 def join_halves(mine, sib):
@@ -313,12 +330,12 @@
         join_out_kernel,
         grid=(rows // 128,),
         out_shape=jax.ShapeDtypeStruct((rows, width), BF16),
-        in_specs=[blk, VMEM],
+        in_specs=[VMEM, VMEM],
         out_specs=blk,
         compiler_params=pltpu.CompilerParams(dimension_semantics=("arbitrary",), vmem_limit_bytes=KEEPING),
         cost_estimate=cost(3 * rows * width, 6 * rows * width),
         name="join_halves",
-    )(mine, in_vmem(sib))
+    )(in_vmem(mine), in_vmem(sib))
 
 
 def weight_grad_kernel(d0_ref, d1_ref, x0_ref, x1_ref, out_ref):
@@ -349,10 +366,10 @@
     def _():
         c = jnp.minimum(step, chunks - 1)
         gate = gate_ref[...]
-        gl = ((gg_ref[...] + gg_sib_ref[...]) * gate * (1.0 - gate)).astype(BF16).astype(F32)[:, :1]
+        gl = ((gg_ref[...] + gg_sib_ref[...]) * (1.0 - gate)).astype(BF16).astype(F32)[:, :1]
         x = x_ref[...].astype(F32)
-        sib = sib_ref[:, pl.ds(pl.multiple_of(c * part, part), part)]
-        back = mine_ref[...].astype(F32) + sib.astype(F32) + gl * rc_ref[:1, :]
+        here = pl.ds(pl.multiple_of(c * part, part), part)
+        back = mine_ref[:, here].astype(F32) + sib_ref[:, here].astype(F32) + gl * rc_ref[:1, :]
         back_ref[...] = back.astype(BF16)
         gain_scr[c] = jnp.sum(x * back, axis=0, keepdims=True)
         router_scr[c] = jnp.sum(x * gl, axis=0, keepdims=True)
@@ -386,13 +403,13 @@
         join_kernel,
         grid=(chunks + 1,),
         out_shape=jax.ShapeDtypeStruct((rows, width + width // CAP + LANES), BF16),
-        in_specs=[col, VMEM] + [whole((rows, LANES))] * 3 + [pl.BlockSpec((CAP, part), at), col],
+        in_specs=[VMEM, VMEM] + [whole((rows, LANES))] * 3 + [pl.BlockSpec((CAP, part), at), col],
         out_specs=pl.BlockSpec((rows, part), lambda i: (0, i)),
         scratch_shapes=[pltpu.VMEM((chunks, 1, part), F32), pltpu.VMEM((chunks, 1, part), F32)],
         compiler_params=pltpu.CompilerParams(dimension_semantics=("arbitrary",), vmem_limit_bytes=KEEPING),
         cost_estimate=cost(10 * rows * width, 8 * rows * width),
         name="join_back",
-    )(mine, in_vmem(sib), gg, gg_sib, gate, rc, x)
+    )(in_vmem(mine), in_vmem(sib), gg, gg_sib, gate, rc, x)
 
 
 def collect_kernel(a_ref, b_ref, c_ref, out_ref):
@@ -416,7 +433,7 @@
         out_shape=jax.ShapeDtypeStruct((CAP + rows // CAP, 2 * LANES), F32),
         in_specs=[lane(0), lane(1), lane(2)],
         out_specs=whole((CAP + rows // CAP, 2 * LANES)),
-        compiler_params=pltpu.CompilerParams(vmem_limit_bytes=KEEPING),
+        compiler_params=pltpu.CompilerParams(vmem_limit_bytes=50 << 20),
         cost_estimate=cost(rows * rows * LANES, 6 * rows * LANES),
         name="collect_sums",
     )(rows_in, rows_in, rows_in)
@@ -499,7 +516,7 @@
         ],
         out_specs=whole((tok_count, width)),
         scratch_shapes=[pltpu.VMEM((tok_count, width), F32)],
-        compiler_params=pltpu.CompilerParams(dimension_semantics=("arbitrary",), vmem_limit_bytes=KEEPING),
+        compiler_params=pltpu.CompilerParams(dimension_semantics=("arbitrary",), vmem_limit_bytes=50 << 20),
         cost_estimate=cost(2 * slots * tok_count * width, 2 * slots * width),
         name="finish_tokens",
     )(place, rows, tokens, gain, upstream)
@@ -529,15 +546,15 @@
     in_1 = across(in_0, CORE, 1)
     gr_1 = across(gr_0, CORE, 1)
 
-    (out_1, hg_1, g_1, u_1, gate_1, _), near = forward(in_1, (wg, wu, wd), True)
-    (out_0, hg_0, g_0, u_0, gate_0, rc), _ = forward(in_0, near, False)
+    (out_1, hg_1, fg_1, fu_1, _, _), near = forward(in_1, (wg, wu, wd), True)
+    (out_0, hg_0, fg_0, fu_0, gate_0, rc), _ = forward(in_0, near, False)
     out_s = across(out_1, CORE, 1)
     out = join_halves(out_0, out_s)
     got_out = in_hbm(exchange(out, experts))
     mixed = mix(place, got_out, tokens)
 
-    (back_1, dg_1, du_1, gg_1), near = backward(gr_1, g_1, u_1, gate_1, (wd, wg, wu), True)
-    (back_0, dg_0, du_0, gg_0), _ = backward(gr_0, g_0, u_0, gate_0, near, False)
+    (back_1, dg_1, du_1, gg_1), near = backward(gr_1, hg_1, fg_1, fu_1, (wd, wg, wu), True)
+    (back_0, dg_0, du_0, gg_0), _ = backward(gr_0, hg_0, fg_0, fu_0, near, False)
     back_s = across(back_1, CORE, 1)
     gg_s = across(gg_1, CORE, 1)
     back = join_back(back_0, back_s, gg_0, gg_s, gate_0, rc, in_0)

time: 238 us -> 239 us (level)
  local copies, waits for them, and re-layouts: 17.3 us -> 25.5 us
  Pallas kernels: 91.5 us -> 84.8 us
    unnamed x36 -> x46, local copies, waits for them, and re-layouts: 16.7 us -> 24.9 us
    pallas_call x2, Pallas kernels: 23.2 us -> 19 us  [backward(): pl.pallas_call(backward_loading_kernel if loading else backward_kernel, g...]
  transfers between devices with their start and end apart: 10 -> 10, of which waited for: 5 -> 5; matrix products, arithmetic and copies ran while one was open for 0% -> 0% of each run, Pallas kernels for 29% -> 27%
where the time goes in v2:
time: 239 us; the launch traced here: 237 us
  Pallas kernels  84.8 us (35%)
  waiting for transfers between devices  79.9 us (33%)
  starting transfers between devices  44.4 us (19%)
  local copies, waits for them, and re-layouts  25.5 us (11%)
    all_to_all x4, waiting for transfers between devices, exchange(): lax.all_to_all(x.reshape(experts, -1, width), CHIPS, 0, 0, tiled=True)  75.8 us
    all_to_all x4, starting transfers between devices, exchange(): lax.all_to_all(x.reshape(experts, -1, width), CHIPS, 0, 0, tiled=True)  35.4 us
    unnamed x46, local copies, waits for them, and re-layouts  24.9 us
    pallas_call x3, Pallas kernels, weight_grad(): pl.pallas_call(weight_grad_kernel, grid=(width // part,), out_shape=jax.S...  21 us
    pallas_call x2, Pallas kernels, forward(): pl.pallas_call(forward_loading_kernel if loading else forward_kernel, gri...  20.6 us
    pallas_call x2, Pallas kernels, backward(): pl.pallas_call(backward_loading_kernel if loading else backward_kernel, g...  19 us
    ppermute x6, starting transfers between devices, across(): return lax.ppermute(block, axis, [(i, i ^ bit) for i in range(count)])  9 us
    pallas_call x1, Pallas kernels, join_back(): pl.pallas_call(join_kernel, grid=(chunks + 1,), out_shape=jax.ShapeDtypeS...  5.17 us
  transfers between devices with their start and end apart: 10, of which 5 were waited for; matrix products, arithmetic and copies ran while one was open for 0% of the time, Pallas kernels for 27%

profile of v2, /device:TPU:1, one launch (start us, length us, event | category | flops | bytes accessed | tf_op | source)
XLA Modules:
  0.0 236.9 jit_solution(1420402402128905003)
XLA Ops:
  0.6 4.6 %dispatch_tokens.1 = (bf16[512,2176]{1,0:T(8,128)(2,1)}, bf16[512,128]{1,0:T(8,128)(2,1)}) custom-call(bf16[128,2048]{1,0:T(8,128)(2,1)} %tok_ref.5, f32[1,2048]{1,0:T(1,128)} %bitcast.34, s32[3,128]{1,0:T(4,128)} %bitcast.53, bf16[64,256]{1,0:T(8,128)(2,1)} %bitcast.52), custom_call_target="tpu_custom_call" | custom-call | flops 268435456 | bytes 4194304 | tf_op jit(solution)/shard_map/dispatch_tokens/pallas_call | solution.py:104
  5.2 11.9 %all-to-all-start = ((bf16[64,8,2176]{2,1,0:T(8,128)(2,1)}), bf16[64,8,2176]{2,1,0:T(8,128)(2,1)S(1)}, u32[]{:S(2)}, u32[]{:S(2)}) async-start(bf16[64,8,2176]{2,1,0:T(8,128)(2,1)} %bitcast.44), calls=%async_computation | async-start | bytes 4456448 | tf_op jit(solution)/shard_map/all_to_all | solution.py:532
  17.2 4.1 %dispatch_grads.1 = bf16[512,2048]{1,0:T(8,128)(2,1)} custom-call(bf16[512,128]{1,0:T(8,128)(2,1)} %get-tuple-element.33.place_ref, bf16[128,2048]{1,0:T(8,128)(2,1)} %up_ref.1), custom_call_target="tpu_custom_call" | custom-call | flops 268435456 | bytes 4194304 | tf_op jit(solution)/shard_map/dispatch_grads/pallas_call | solution.py:132
  21.2 24.7 %all-to-all-done = bf16[64,8,2176]{2,1,0:T(8,128)(2,1)S(1)} async-done(((bf16[64,8,2176]{2,1,0:T(8,128)(2,1)}), bf16[64,8,2176]{2,1,0:T(8,128)(2,1)S(1)}, u32[]{:S(2)}, u32[]{:S(2)}) %all-to-all-start) | async-done | bytes 2228256 | tf_op jit(solution)/shard_map/all_to_all | solution.py:532
  45.9 7.8 %all-to-all-start.2 = ((bf16[64,8,2048]{2,1,0:T(8,128)(2,1)}), bf16[64,8,2048]{2,1,0:T(8,128)(2,1)}, u32[]{:S(2)}, u32[]{:S(2)}) async-start(bf16[64,8,2048]{2,1,0:T(8,128)(2,1)} %bitcast.43), calls=%async_computation.2 | async-start | bytes 4194304 | tf_op jit(solution)/shard_map/all_to_all | solution.py:532
  53.7 2.4 %collective-permute-start = (bf16[512,2176]{1,0:T(8,128)(2,1)}, bf16[512,2176]{1,0:T(8,128)(2,1)S(1)}, u32[]{:S(2)}, u32[]{:S(2)}) collective-permute-start(bf16[512,2176]{1,0:T(8,128)(2,1)} %bitcast.37), channel_id=1, source_target_pairs={{0,1},{1,0},{2,3},{3,2},{4,5},{5,4},{6,7},{7,6},{8,9},{9,8},{10,11... | collective-permute-start | bytes 6684680 | tf_op jit(solution)/shard_map/ppermute | solution.py:527
  56.1 23.4 %all-to-all-done.2 = bf16[64,8,2048]{2,1,0:T(8,128)(2,1)} async-done(((bf16[64,8,2048]{2,1,0:T(8,128)(2,1)}), bf16[64,8,2048]{2,1,0:T(8,128)(2,1)}, u32[]{:S(2)}, u32[]{:S(2)}) %all-to-all-start.2) | async-done | bytes 2097184 | tf_op jit(solution)/shard_map/all_to_all | solution.py:532
  79.5 4.3 %collective-permute-start.2 = (bf16[512,2048]{1,0:T(8,128)(2,1)}, bf16[512,2048]{1,0:T(8,128)(2,1)S(1)}, u32[]{:S(2)}, u32[]{:S(2)}) collective-permute-start(bf16[512,2048]{1,0:T(8,128)(2,1)} %bitcast.13.gr.x0_ref), channel_id=1, source_target_pairs={{0,1},{1,0},{2,3},{3,2},{4,5},{5,4},{6,7},{7,6},{8,9},{9,8},{10,11... | collective-permute-start | bytes 6291464 | tf_op jit(solution)/shard_map/ppermute | solution.py:527
  83.8 11.4 %expert_forward.2 = (bf16[512,2048]{1,0:T(8,128)(2,1)}, bf16[512,704]{1,0:T(8,128)(2,1)}, bf16[512,704]{1,0:T(8,128)(2,1)}, bf16[512,704]{1,0:T(8,128)(2,1)}, f3...) custom-call(bf16[512,2176]{1,0:T(8,128)(2,1)S(1)} %collective-permut, ...), custom_call_target="tpu_custom_call" | custom-call | flops 4429185024 | bytes 17039360 | tf_op jit(solution)/shard_map/expert_forward/pallas_call | solution.py:227
  100.0 10.5 %expert_backward.2 = (bf16[512,2048]{1,0:T(8,128)(2,1)}, bf16[512,704]{1,0:T(8,128)(2,1)}, bf16[512,704]{1,0:T(8,128)(2,1)}, f32[512,128]{1,0:T(8,128)}, bf16[70...) custom-call(bf16[512,2048]{1,0:T(8,128)(2,1)S(1)} %collective-permute-done.2.gr.x1_ref, ...), custom_call_target="tpu_custom_call" | custom-call | flops 4429185024 | bytes 17039360 | tf_op jit(solution)/shard_map/expert_backward/pallas_call | solution.py:303
  121.2 9.2 %expert_forward.3 = (bf16[512,2048]{1,0:T(8,128)(2,1)S(1)}, bf16[512,704]{1,0:T(8,128)(2,1)}, bf16[512,704]{1,0:T(8,128)(2,1)}, bf16[512,704]{1,0:T(8,128)(2,1)}, f32[512,128]{1,0:T(8,128)}, /*index=5*/f32[8,2048]{1,0:T(8,128)}) custom-call(bf16[512,2176]{1,0:T(8,128)(2,1)} %bitcast.38, bf16[704,2048]{1,0:T(8,128)(2,1)S(1)} %copy-done.15, ...), custom_call_target="tpu_custom_call" | custom-call | flops 4429185024 | bytes 17039360 | tf_op jit(solution)/shard_map/expert_forward/pallas_call | solution.py:227
  137.2 8.5 %expert_backward.3 = (bf16[512,2048]{1,0:T(8,128)(2,1)S(1)}, bf16[512,704]{1,0:T(8,128)(2,1)}, bf16[512,704]{1,0:T(8,128)(2,1)}, f32[512,128]{1,0:T(8,128)}) custom-call(bf16[512,2048]{1,0:T(8,128)(2,1)} %bitcast.13.gr.x0_ref, bf16[512,704]{1,0:T(8,128)(2,1)} %get-tuple-element.40.hg.d0_ref, bf16[512,704]{1,0:T(8,128)(2,1)} %get-tuple-element.41.fg, ...), custom_call_target="tpu_custom_call" | custom-call | flops 4429185024 | bytes 17039360 | tf_op jit(solution)/shard_map/expert_backward/pallas_call | solution.py:303
  146.4 5.2 %join_back.1 = bf16[512,2432]{1,0:T(8,128)(2,1)} custom-call(bf16[512,2048]{1,0:T(8,128)(2,1)S(1)} %get-tuple-element.49.mine_ref, bf16[512,2048]{1,0:T(8,128)(2,1)S(1)} %collective-permute-done.3.sib_ref, f32[512,128]{1,0:T(8,128)} %get-tuple-element.51.gg_ref, f32[512,128]{1,0:T(8,128)} %copy-done.21, f32[512,128]{1,0:T(8,128)} %get-tuple-element.53.gate_ref, ...), custom_call_target="tpu_custom_call" | custom-call | flops 10485760 | bytes 8388608 | tf_op jit(solution)/shard_map/join_back/pallas_call | solution.py:402
  151.5 6.1 %all-to-all-start.3 = ((bf16[64,8,2432]{2,1,0:T(8,128)(2,1)}), bf16[64,8,2432]{2,1,0:T(8,128)(2,1)S(1)}, u32[]{:S(2)}, u32[]{:S(2)}) async-start(bf16[64,8,2432]{2,1,0:T(8,128)(2,1)} %bitcast.36), calls=%async_computation.3 | async-start | bytes 4980736 | tf_op jit(solution)/shard_map/all_to_all | solution.py:532
  158.0 4.1 %collective-permute-done.1.sib_ref = bf16[512,2048]{1,0:T(8,128)(2,1)S(1)} collective-permute-done((bf16[512,2048]{1,0:T(8,128)(2,1)}, bf16[512,2048]{1,0:T(8,128)(2,1)S(1)}, u32[]{:S(2)}, u32[]{:S(2)}) %collective-permute-start.1) | collective-permute-done | bytes 2097184 | tf_op jit(solution)/shard_map/ppermute | solution.py:527
  163.7 2.0 join_halves.1
  165.8 24.0 %all-to-all-done.3 = bf16[64,8,2432]{2,1,0:T(8,128)(2,1)S(1)} async-done(((bf16[64,8,2432]{2,1,0:T(8,128)(2,1)}), bf16[64,8,2432]{2,1,0:T(8,128)(2,1)S(1)}, u32[]{:S(2)}, u32[]{:S(2)}) %all-to-all-start.3) | async-done | bytes 2490400 | tf_op jit(solution)/shard_map/all_to_all | solution.py:532
  189.8 9.5 %all-to-all-start.1 = ((bf16[64,8,2048]{2,1,0:T(8,128)(2,1)}), bf16[64,8,2048]{2,1,0:T(8,128)(2,1)}, u32[]{:S(2)}, u32[]{:S(2)}) async-start(bf16[64,8,2048]{2,1,0:T(8,128)(2,1)} %bitcast.42), calls=%async_computation.1 | async-start | bytes 4194304 | tf_op jit(solution)/shard_map/all_to_all | solution.py:532
  199.3 7.0 %shard_map.137 = bf16[704,2048]{1,0:T(8,128)(2,1)} custom-call(bf16[512,704]{1,0:T(8,128)(2,1)} %get-tuple-element.40.hg.d0_ref, bf16[512,704]{1,0:T(8,128)(2,1)} %get-tuple-element.43.hg.d1_ref, bf16[512,2048]{1,0:T(8,128)(2,1)} %bitcast.13.gr.x0_ref, bf16[512,2048]{1,0:T(8,128)(2,1)} %copy-done.7), custom_call_target="tpu_custom_call" | custom-call | flops 2952790016 | bytes 7077888 | tf_op jit(solution)/shard_map/pallas_call | solution.py:349
  206.3 7.0 %shard_map.135 = bf16[704,2048]{1,0:T(8,128)(2,1)} custom-call(bf16[512,704]{1,0:T(8,128)(2,1)} %get-tuple-element.55.d0_ref, bf16[512,704]{1,0:T(8,128)(2,1)} %get-tuple-element.56.d1_ref, bf16[512,2176]{1,0:T(8,128)(2,1)} %bitcast.40, bf16[512,2176]{1,0:T(8,128)(2,1)} %copy-done.6), custom_call_target="tpu_custom_call" | custom-call | flops 2952790016 | bytes 7077888 | tf_op jit(solution)/shard_map/pallas_call | solution.py:349
  215.5 7.0 %shard_map.136 = bf16[704,2048]{1,0:T(8,128)(2,1)} custom-call(bf16[512,704]{1,0:T(8,128)(2,1)} %get-tuple-element.57.d0_ref, bf16[512,704]{1,0:T(8,128)(2,1)} %get-tuple-element.58.d1_ref, bf16[512,2176]{1,0:T(8,128)(2,1)} %bitcast.41, bf16[512,2176]{1,0:T(8,128)(2,1)} %copy-done.6), custom_call_target="tpu_custom_call" | custom-call | flops 2952790016 | bytes 7077888 | tf_op jit(solution)/shard_map/pallas_call | solution.py:349
  222.5 3.7 %all-to-all-done.1 = bf16[64,8,2048]{2,1,0:T(8,128)(2,1)} async-done(((bf16[64,8,2048]{2,1,0:T(8,128)(2,1)}), bf16[64,8,2048]{2,1,0:T(8,128)(2,1)}, u32[]{:S(2)}, u32[]{:S(2)}) %all-to-all-start.1) | async-done | bytes 2097184 | tf_op jit(solution)/shard_map/all_to_all | solution.py:532
  226.3 4.5 %mix_outputs.1 = bf16[128,2048]{1,0:T(8,128)(2,1)} custom-call(bf16[512,128]{1,0:T(8,128)(2,1)} %get-tuple-element.33.place_ref, bf16[512,2048]{1,0:T(8,128)(2,1)} %bitcast.11.rows_ref, bf16[128,2048]{1,0:T(8,128)(2,1)} %tok_ref.5), custom_call_target="tpu_custom_call" | custom-call | flops 268435456 | bytes 2097152 | tf_op jit(solution)/shard_map/mix_outputs/pallas_call | solution.py:463
  231.6 3.1 %finish_tokens.1 = bf16[128,2048]{1,0:T(8,128)(2,1)} custom-call(bf16[512,128]{1,0:T(8,128)(2,1)S(1)} %copy-done.4, bf16[512,2432]{1,0:T(8,128)(2,1)S(1)} %bitcast.33, bf16[128,2048]{1,0:T(8,128)(2,1)S(1)} %copy-done.2, f32[1,2048]{1,0:T(1,128)S(1)} %bitcast.35, bf16[128,2048]{1,0:T(8,128)(2,1)S(1)} %copy-done.3), custom_call_target="tpu_custom_call" | custom-call | flops 268435456 | bytes 2097152 | tf_op jit(solution)/shard_map/finish_tokens/pallas_call | solution.py:506
  (59 shorter events, 30.2 us)
Async XLA Ops:
  5.2 40.7 %all-to-all-start = ((bf16[64,8,2176]{2,1,0:T(8,128)(2,1)}), bf16[64,8,2176]{2,1,0:T(8,128)(2,1)S(1)}, u32[]{:S(2)}, u32[]{:S(2)}) async-start(bf16[64,8,2176]{2,1,0:T(8,128)(2,1)} %bitcast.44), calls=%async_computation | async-start | bytes 4456448 | tf_op jit(solution)/shard_map/all_to_all | solution.py:532
  45.9 7.8 %copy-start.20 = (bf16[64,8,2176]{2,1,0:T(8,128)(2,1)}, bf16[64,8,2176]{2,1,0:T(8,128)(2,1)S(1)}, u32[]{:S(2)}) copy-start(bf16[64,8,2176]{2,1,0:T(8,128)(2,1)S(1)} %all-to-all-done) | copy-start | bytes 6684676
  45.9 33.6 %all-to-all-start.2 = ((bf16[64,8,2048]{2,1,0:T(8,128)(2,1)}), bf16[64,8,2048]{2,1,0:T(8,128)(2,1)}, u32[]{:S(2)}, u32[]{:S(2)}) async-start(bf16[64,8,2048]{2,1,0:T(8,128)(2,1)} %bitcast.43), calls=%async_computation.2 | async-start | bytes 4194304 | tf_op jit(solution)/shard_map/all_to_all | solution.py:532
  53.7 30.1 %collective-permute-start = (bf16[512,2176]{1,0:T(8,128)(2,1)}, bf16[512,2176]{1,0:T(8,128)(2,1)S(1)}, u32[]{:S(2)}, u32[]{:S(2)}) collective-permute-start(bf16[512,2176]{1,0:T(8,128)(2,1)} %bitcast.37), channel_id=1, source_target_pairs={{0,1},{1,0},{2,3},{3,2},{4,5},{5,4},{6,7},{7,6},{8,9},{9,8},{10,11... | collective-permute-start | bytes 6684680 | tf_op jit(solution)/shard_map/ppermute | solution.py:527
  79.5 20.5 %collective-permute-start.2 = (bf16[512,2048]{1,0:T(8,128)(2,1)}, bf16[512,2048]{1,0:T(8,128)(2,1)S(1)}, u32[]{:S(2)}, u32[]{:S(2)}) collective-permute-start(bf16[512,2048]{1,0:T(8,128)(2,1)} %bitcast.13.gr.x0_ref), channel_id=1, source_target_pairs={{0,1},{1,0},{2,3},{3,2},{4,5},{5,4},{6,7},{7,6},{8,9},{9,8},{10,11... | collective-permute-start | bytes 6291464 | tf_op jit(solution)/shard_map/ppermute | solution.py:527
  83.8 11.4 %copy-start.6 = (bf16[512,2176]{1,0:T(8,128)(2,1)}, bf16[512,2176]{1,0:T(8,128)(2,1)S(1)}, u32[]{:S(2)}) copy-start(bf16[512,2176]{1,0:T(8,128)(2,1)S(1)} %collective-permute-done.x_hbm.x1_ref) | copy-start | bytes 6684676
  100.0 10.5 %copy-start.7 = (bf16[512,2048]{1,0:T(8,128)(2,1)}, bf16[512,2048]{1,0:T(8,128)(2,1)S(1)}, u32[]{:S(2)}) copy-start(bf16[512,2048]{1,0:T(8,128)(2,1)S(1)} %collective-permute-done.2.gr.x1_ref) | copy-start | bytes 6291460
  112.0 1.6 copy-start.10
  113.6 1.6 copy-start.12
  115.3 30.4 %collective-permute-start.3 = (bf16[512,2048]{1,0:T(8,128)(2,1)}, bf16[512,2048]{1,0:T(8,128)(2,1)S(1)}, u32[]{:S(2)}, u32[]{:S(2)}) collective-permute-start(bf16[512,2048]{1,0:T(8,128)(2,1)} %get-tuple-element.50), channel_id=1, source_target_pairs={{0,1},{1,0},{2,3},{3,2},{4,5},{5,4},{6,7},{7,6},{8,9},{9,8},{10,11... | collective-permute-start | bytes 6291464 | tf_op jit(solution)/shard_map/ppermute | solution.py:527
  115.3 30.4 %collective-permute-start.4 = (f32[512,128]{1,0:T(8,128)}, f32[512,128]{1,0:T(8,128)S(1)}, u32[]{:S(2)}, u32[]{:S(2)}) collective-permute-start(f32[512,128]{1,0:T(8,128)} %get-tuple-element.52), channel_id=1, source_target_pairs={{0,1},{1,0},{2,3},{3,2},{4,5},{5,4},{6,7},{7,6},{8,9},{9,8},{10,11... | collective-permute-start | bytes 786440 | tf_op jit(solution)/shard_map/ppermute | solution.py:527
  115.8 1.8 copy-start.15
  117.6 1.8 copy-start.17
  119.4 1.8 copy-start.19
  131.7 1.8 copy-start.9
  133.6 1.8 copy-start.11
  135.4 1.8 copy-start.13
  151.5 38.2 %all-to-all-start.3 = ((bf16[64,8,2432]{2,1,0:T(8,128)(2,1)}), bf16[64,8,2432]{2,1,0:T(8,128)(2,1)S(1)}, u32[]{:S(2)}, u32[]{:S(2)}) async-start(bf16[64,8,2432]{2,1,0:T(8,128)(2,1)} %bitcast.36), calls=%async_computation.3 | async-start | bytes 4980736 | tf_op jit(solution)/shard_map/all_to_all | solution.py:532
  157.7 4.5 %collective-permute-start.1 = (bf16[512,2048]{1,0:T(8,128)(2,1)}, bf16[512,2048]{1,0:T(8,128)(2,1)S(1)}, u32[]{:S(2)}, u32[]{:S(2)}) collective-permute-start(bf16[512,2048]{1,0:T(8,128)(2,1)} %get-tuple-element.39), channel_id=1, source_target_pairs={{0,1},{1,0},{2,3},{3,2},{4,5},{5,4},{6,7},{7,6},{8,9},{9,8},{10,11... | collective-permute-start | bytes 6291464 | tf_op jit(solution)/shard_map/ppermute | solution.py:527
  189.8 36.5 %all-to-all-start.1 = ((bf16[64,8,2048]{2,1,0:T(8,128)(2,1)}), bf16[64,8,2048]{2,1,0:T(8,128)(2,1)}, u32[]{:S(2)}, u32[]{:S(2)}) async-start(bf16[64,8,2048]{2,1,0:T(8,128)(2,1)} %bitcast.42), calls=%async_computation.1 | async-start | bytes 4194304 | tf_op jit(solution)/shard_map/all_to_all | solution.py:532
  214.2 20.6 %collective-permute-start.5 = (f32[72,256]{1,0:T(8,128)}, f32[72,256]{1,0:T(8,128)}, u32[]{:S(2)}, u32[]{:S(2)}) collective-permute-start(f32[72,256]{1,0:T(8,128)} %collect_sums.1), channel_id=1, source_target_pairs={{0,1},{1,0},{2,3},{3,2},{4,5},{5,4},{6,7},{7,6},{8,9},{9,8},{10,11... | collective-permute-start | bytes 221192 | tf_op jit(solution)/shard_map/ppermute | solution.py:527
  222.5 8.2 %copy-start.2 = (bf16[128,2048]{1,0:T(8,128)(2,1)S(1)}, bf16[128,2048]{1,0:T(8,128)(2,1)}, u32[]{:S(2)}) copy-start(bf16[128,2048]{1,0:T(8,128)(2,1)} %tok_ref.5) | copy-start | bytes 1572868
  222.5 8.2 %copy-start.3 = (bf16[128,2048]{1,0:T(8,128)(2,1)S(1)}, bf16[128,2048]{1,0:T(8,128)(2,1)}, u32[]{:S(2)}) copy-start(bf16[128,2048]{1,0:T(8,128)(2,1)} %up_ref.1) | copy-start | bytes 1572868
  222.5 8.2 %copy-start.5 = (f32[2048]{0:T(1024)S(1)}, f32[2048]{0:T(1024)}, u32[]{:S(2)}) copy-start(f32[2048]{0:T(1024)} %param.9) | copy-start | bytes 24580
  (8 other events, 10.8 us)

commit v3 on v2

--- a/solution.py
+++ b/solution.py
@@ -57,63 +57,61 @@
     return jnp.where(column_of(row) == col, 1.0, 0.0).astype(BF16)
 
 
-def dispatch_kernel(tok_ref, gain_ref, ids_ref, router_ref, send_ref, place_ref, scaled_scr):
-    step = pl.program_id(0)
-    chunks, tok_count, width = scaled_scr.shape
+def dispatch_kernel(tok_ref, gain_ref, ids_ref, router_ref, send_hbm, place_ref, send, sems):
+    tok_count, width = tok_ref.shape
     slots = place_ref.shape[0]
     experts = slots // CAP
-
-    @pl.when(step == 0)
-    def _():
-        x = tok_ref[...].astype(F32)
-        inverse = lax.rsqrt(jnp.mean(x * x, axis=1, keepdims=True) + EPSILON)
-        scaled = (x * inverse * gain_ref[...]).astype(BF16)
-        for c in range(chunks):
-            scaled_scr[c] = scaled[:, c * width : (c + 1) * width]
-        ids = ids_ref[...]
-        expert = lax.broadcasted_iota(jnp.int32, (experts, tok_count), 0)
-        named = jnp.zeros((experts, tok_count), F32)
-        for k in range(ids.shape[0]):
-            named = named + jnp.where(ids[k : k + 1, :] == expert, 1.0, 0.0)
-        before = lax.broadcasted_iota(jnp.int32, (tok_count, tok_count), 0)
-        after = lax.broadcasted_iota(jnp.int32, (tok_count, tok_count), 1)
-        earlier = jnp.where(before < after, 1.0, 0.0).astype(BF16)
-        rank = dot_nn(named.astype(BF16), earlier)
-        order = (named * (rank + 1.0)).astype(BF16)
-        order_of = dot_nn(one_hot_rows(slots, experts, lambda row: row // CAP), order)
-        want = (lax.broadcasted_iota(jnp.int32, (slots, tok_count), 0) % CAP + 1).astype(F32)
-        place_ref[...] = jnp.where(order_of == want, 1.0, 0.0).astype(BF16)
-
-    @pl.when(step < chunks)
-    def _():
-        send_ref[...] = dot_nn(place_ref[...], scaled_scr[jnp.minimum(step, chunks - 1)]).astype(BF16)
-
-    @pl.when(step == chunks)
-    def _():
-        extra = jnp.zeros((slots, LANES), F32)
-        for j in range(router_ref.shape[1] // LANES):
-            pick = one_hot_rows(slots, experts, lambda row: jnp.where(row % CAP == j, row // CAP, -1))
-            extra = extra + dot_nn(pick, router_ref[:, j * LANES : (j + 1) * LANES])
-        send_ref[:, :LANES] = extra.astype(BF16)
+    puts = []
+
+    def put(lo, hi):
+        copy = pltpu.make_async_copy(send.at[:, lo:hi], send_hbm.at[:, lo:hi], sems.at[len(puts)])
+        copy.start()
+        puts.append(copy)
+
+    ids = ids_ref[...]
+    expert = lax.broadcasted_iota(jnp.int32, (experts, tok_count), 0)
+    named = jnp.zeros((experts, tok_count), F32)
+    for k in range(ids.shape[0]):
+        named = named + jnp.where(ids[k : k + 1, :] == expert, 1.0, 0.0)
+    before = lax.broadcasted_iota(jnp.int32, (tok_count, tok_count), 0)
+    after = lax.broadcasted_iota(jnp.int32, (tok_count, tok_count), 1)
+    earlier = jnp.where(before < after, 1.0, 0.0).astype(BF16)
+    rank = dot_nn(named.astype(BF16), earlier)
+    order = (named * (rank + 1.0)).astype(BF16)
+    order_of = dot_nn(one_hot_rows(slots, experts, lambda row: row // CAP), order)
+    want = (lax.broadcasted_iota(jnp.int32, (slots, tok_count), 0) % CAP + 1).astype(F32)
+    place = jnp.where(order_of == want, 1.0, 0.0).astype(BF16)
+    place_ref[...] = place
+    extra = jnp.zeros((slots, LANES), F32)
+    for j in range(router_ref.shape[1] // LANES):
+        pick = one_hot_rows(slots, experts, lambda row: jnp.where(row % CAP == j, row // CAP, -1))
+        extra = extra + dot_nn(pick, router_ref[:, j * LANES : (j + 1) * LANES])
+    send[:, width:] = extra.astype(BF16)
+    put(width, width + LANES)
+    x = tok_ref[...].astype(F32)
+    inverse = lax.rsqrt(jnp.mean(x * x, axis=1, keepdims=True) + EPSILON)
+    part = width // CHUNKS
+    for c in range(CHUNKS):
+        cols = slice(c * part, (c + 1) * part)
+        scaled = (tok_ref[:, cols].astype(F32) * inverse * gain_ref[:, cols]).astype(BF16)
+        send[:, cols] = dot_nn(place, scaled).astype(BF16)
+        put(c * part, (c + 1) * part)
+    for copy in puts:
+        copy.wait()
 
 
 def dispatch(tokens, gain, ids, router, slots):
     tok_count, width = tokens.shape
-    chunks = 4
-    part = width // chunks
     return pl.pallas_call(
         dispatch_kernel,
-        grid=(chunks + 1,),
+        grid=(1,),
         out_shape=(
             jax.ShapeDtypeStruct((slots, width + LANES), BF16),
             jax.ShapeDtypeStruct((slots, tok_count), BF16),
         ),
         in_specs=[whole((tok_count, width)), whole((1, width)), whole(ids.shape), whole(router.shape)],
-        out_specs=(
-            pl.BlockSpec((slots, part), lambda i: (0, i)),
-            whole((slots, tok_count)),
-        ),
-        scratch_shapes=[pltpu.VMEM((chunks, tok_count, part), BF16)],
+        out_specs=(HBM, whole((slots, tok_count))),
+        scratch_shapes=[pltpu.VMEM((slots, width + LANES), BF16), pltpu.SemaphoreType.DMA((1 + CHUNKS,))],
         compiler_params=pltpu.CompilerParams(dimension_semantics=("arbitrary",)),
         cost_estimate=cost(2 * slots * tok_count * width, 2 * slots * width * 2),
         name="dispatch_tokens",
@@ -366,13 +364,14 @@
     def _():
         c = jnp.minimum(step, chunks - 1)
         gate = gate_ref[...]
-        gl = ((gg_ref[...] + gg_sib_ref[...]) * (1.0 - gate)).astype(BF16).astype(F32)[:, :1]
+        gl_wide = ((gg_ref[...] + gg_sib_ref[...]) * (1.0 - gate)).astype(BF16)
+        gl = gl_wide.astype(F32)[:, :1]
         x = x_ref[...].astype(F32)
         here = pl.ds(pl.multiple_of(c * part, part), part)
         back = mine_ref[:, here].astype(F32) + sib_ref[:, here].astype(F32) + gl * rc_ref[:1, :]
         back_ref[...] = back.astype(BF16)
         gain_scr[c] = jnp.sum(x * back, axis=0, keepdims=True)
-        router_scr[c] = jnp.sum(x * gl, axis=0, keepdims=True)
+        router_scr[c] = dot_tn(gl_wide, x_ref[...])[:1, :]
 
     @pl.when(step == chunks)
     def _():
@@ -403,13 +402,13 @@
         join_kernel,
         grid=(chunks + 1,),
         out_shape=jax.ShapeDtypeStruct((rows, width + width // CAP + LANES), BF16),
-        in_specs=[VMEM, VMEM] + [whole((rows, LANES))] * 3 + [pl.BlockSpec((CAP, part), at), col],
+        in_specs=[VMEM, VMEM, whole((rows, LANES)), VMEM, whole((rows, LANES))] + [pl.BlockSpec((CAP, part), at), col],
         out_specs=pl.BlockSpec((rows, part), lambda i: (0, i)),
         scratch_shapes=[pltpu.VMEM((chunks, 1, part), F32), pltpu.VMEM((chunks, 1, part), F32)],
         compiler_params=pltpu.CompilerParams(dimension_semantics=("arbitrary",), vmem_limit_bytes=KEEPING),
         cost_estimate=cost(10 * rows * width, 8 * rows * width),
         name="join_back",
-    )(in_vmem(mine), in_vmem(sib), gg, gg_sib, gate, rc, x)
+    )(in_vmem(mine), in_vmem(sib), gg, in_vmem(gg_sib), gate, rc, x)
 
 
 def collect_kernel(a_ref, b_ref, c_ref, out_ref):
@@ -437,6 +436,30 @@
         cost_estimate=cost(rows * rows * LANES, 6 * rows * LANES),
         name="collect_sums",
     )(rows_in, rows_in, rows_in)
+
+
+def total_kernel(mine_ref, sib_ref, gain_ref, gain_out_ref, router_ref):
+    total = mine_ref[...] + sib_ref[...]
+    router_ref[...] = total[CAP:, :]
+    row = jnp.concatenate([total[j : j + 1, :] for j in range(CAP)], axis=1)
+    gain_out_ref[...] = row / gain_ref[...]
+
+
+def total_sums(mine, sib, gain):
+    rows, part = mine.shape
+    return pl.pallas_call(
+        total_kernel,
+        grid=(1,),
+        out_shape=(
+            jax.ShapeDtypeStruct(gain.shape, F32),
+            jax.ShapeDtypeStruct((rows - CAP, part), F32),
+        ),
+        in_specs=[VMEM, VMEM, whole(gain.shape)],
+        out_specs=(whole(gain.shape), whole((rows - CAP, part))),
+        compiler_params=pltpu.CompilerParams(vmem_limit_bytes=50 << 20),
+        cost_estimate=cost(2 * mine.size, 12 * mine.size),
+        name="total_sums",
+    )(in_vmem(mine), in_vmem(sib), gain)
 
 
 def mix_kernel(place_ref, rows_ref, tok_ref, mixed_ref, acc_ref):
@@ -566,14 +589,13 @@
     grad_up = weight_grad(du_0, du_1, in_0, in_1, width)
 
     sums = collect(got_back, width)
-    sums = sums + across(sums, CORE, 1)
-    grad_gain = sums[:CAP].reshape(width) / norm_gain
-    grad_router = sums[CAP:].T
+    sums_s = across(sums, CORE, 1)
+    grad_gain, grad_router = total_sums(sums, sums_s, gain)
     return (
         mixed,
         grad_tokens,
-        grad_gain,
-        grad_router,
+        grad_gain.reshape(width),
+        grad_router.T,
         grad_gate.T[None],
         grad_up.T[None],
         grad_down[None],

time: 239 us -> 237 us (level)
    unnamed x46 -> x42, local copies, waits for them, and re-layouts: 24.9 us -> 24.2 us
    pallas_call x1 -> x2, Pallas kernels: 4.6 us -> 5.2 us  [the longest x1 3.64 us: dispatch(): pl.pallas_call(dispatch_kernel, grid=(1,), out_shape=(jax.ShapeDtypeStruc...]
where the time goes in v3:
time: 237 us; the launch traced here: 235 us
  Pallas kernels  85.3 us (36%)
  waiting for transfers between devices  79.9 us (34%)
  starting transfers between devices  44.5 us (19%)
  local copies, waits for them, and re-layouts  24.2 us (10%)
    all_to_all x4, waiting for transfers between devices, exchange(): lax.all_to_all(x.reshape(experts, -1, width), CHIPS, 0, 0, tiled=True)  75.8 us
    all_to_all x4, starting transfers between devices, exchange(): lax.all_to_all(x.reshape(experts, -1, width), CHIPS, 0, 0, tiled=True)  35.5 us
    unnamed x42, local copies, waits for them, and re-layouts  24.2 us
    pallas_call x3, Pallas kernels, weight_grad(): pl.pallas_call(weight_grad_kernel, grid=(width // part,), out_shape=jax.S...  21 us
    pallas_call x2, Pallas kernels, forward(): pl.pallas_call(forward_loading_kernel if loading else forward_kernel, gri...  20.6 us
    pallas_call x2, Pallas kernels, backward(): pl.pallas_call(backward_loading_kernel if loading else backward_kernel, g...  19 us
    ppermute x6, starting transfers between devices, across(): return lax.ppermute(block, axis, [(i, i ^ bit) for i in range(count)])  9.05 us
    pallas_call x1, Pallas kernels, join_back(): pl.pallas_call(join_kernel, grid=(chunks + 1,), out_shape=jax.ShapeDtypeS...  5.1 us
  transfers between devices with their start and end apart: 10, of which 5 were waited for; matrix products, arithmetic and copies ran while one was open for 0% of the time, Pallas kernels for 27%

profile of v3, /device:TPU:1, one launch (start us, length us, event | category | flops | bytes accessed | tf_op | source)
XLA Modules:
  0.0 234.7 jit_solution(198229975128071347)
XLA Ops:
  0.6 3.6 %dispatch_tokens.1 = (bf16[512,2176]{1,0:T(8,128)(2,1)}, bf16[512,128]{1,0:T(8,128)(2,1)}) custom-call(bf16[128,2048]{1,0:T(8,128)(2,1)} %tok_ref.5, f32[1,2048]{1,0:T(1,128)} %bitcast.31, s32[3,128]{1,0:T(4,128)} %bitcast.52, bf16[64,256]{1,0:T(8,128)(2,1)} %bitcast.50), custom_call_target="tpu_custom_call" | custom-call | flops 268435456 | bytes 4194304 | tf_op jit(solution)/shard_map/dispatch_tokens/pallas_call | solution.py:105
  4.3 12.0 %all-to-all-start = ((bf16[64,8,2176]{2,1,0:T(8,128)(2,1)}), bf16[64,8,2176]{2,1,0:T(8,128)(2,1)S(1)}, u32[]{:S(2)}, u32[]{:S(2)}) async-start(bf16[64,8,2176]{2,1,0:T(8,128)(2,1)} %bitcast.42), calls=%async_computation | async-start | bytes 4456448 | tf_op jit(solution)/shard_map/all_to_all | solution.py:555
  16.3 4.0 %dispatch_grads.1 = bf16[512,2048]{1,0:T(8,128)(2,1)} custom-call(bf16[512,128]{1,0:T(8,128)(2,1)} %get-tuple-element.35.place_ref, bf16[128,2048]{1,0:T(8,128)(2,1)} %up_ref.1), custom_call_target="tpu_custom_call" | custom-call | flops 268435456 | bytes 4194304 | tf_op jit(solution)/shard_map/dispatch_grads/pallas_call | solution.py:130
  20.3 24.7 %all-to-all-done = bf16[64,8,2176]{2,1,0:T(8,128)(2,1)S(1)} async-done(((bf16[64,8,2176]{2,1,0:T(8,128)(2,1)}), bf16[64,8,2176]{2,1,0:T(8,128)(2,1)S(1)}, u32[]{:S(2)}, u32[]{:S(2)}) %all-to-all-start) | async-done | bytes 2228256 | tf_op jit(solution)/shard_map/all_to_all | solution.py:555
  45.0 7.8 %all-to-all-start.2 = ((bf16[64,8,2048]{2,1,0:T(8,128)(2,1)}), bf16[64,8,2048]{2,1,0:T(8,128)(2,1)}, u32[]{:S(2)}, u32[]{:S(2)}) async-start(bf16[64,8,2048]{2,1,0:T(8,128)(2,1)} %bitcast.41), calls=%async_computation.2 | async-start | bytes 4194304 | tf_op jit(solution)/shard_map/all_to_all | solution.py:555
  52.8 2.4 %collective-permute-start = (bf16[512,2176]{1,0:T(8,128)(2,1)}, bf16[512,2176]{1,0:T(8,128)(2,1)S(1)}, u32[]{:S(2)}, u32[]{:S(2)}) collective-permute-start(bf16[512,2176]{1,0:T(8,128)(2,1)} %bitcast.35), channel_id=1, source_target_pairs={{0,1},{1,0},{2,3},{3,2},{4,5},{5,4},{6,7},{7,6},{8,9},{9,8},{10,11... | collective-permute-start | bytes 6684680 | tf_op jit(solution)/shard_map/ppermute | solution.py:550
  55.2 23.3 %all-to-all-done.2 = bf16[64,8,2048]{2,1,0:T(8,128)(2,1)} async-done(((bf16[64,8,2048]{2,1,0:T(8,128)(2,1)}), bf16[64,8,2048]{2,1,0:T(8,128)(2,1)}, u32[]{:S(2)}, u32[]{:S(2)}) %all-to-all-start.2) | async-done | bytes 2097184 | tf_op jit(solution)/shard_map/all_to_all | solution.py:555
  78.5 4.4 %collective-permute-start.2 = (bf16[512,2048]{1,0:T(8,128)(2,1)}, bf16[512,2048]{1,0:T(8,128)(2,1)S(1)}, u32[]{:S(2)}, u32[]{:S(2)}) collective-permute-start(bf16[512,2048]{1,0:T(8,128)(2,1)} %bitcast.13.gr.x0_ref), channel_id=1, source_target_pairs={{0,1},{1,0},{2,3},{3,2},{4,5},{5,4},{6,7},{7,6},{8,9},{9,8},{10,11... | collective-permute-start | bytes 6291464 | tf_op jit(solution)/shard_map/ppermute | solution.py:550
  82.9 11.4 %expert_forward.2 = (bf16[512,2048]{1,0:T(8,128)(2,1)}, bf16[512,704]{1,0:T(8,128)(2,1)}, bf16[512,704]{1,0:T(8,128)(2,1)}, bf16[512,704]{1,0:T(8,128)(2,1)}, f3...) custom-call(bf16[512,2176]{1,0:T(8,128)(2,1)S(1)} %collective-permut, ...), custom_call_target="tpu_custom_call" | custom-call | flops 4429185024 | bytes 17039360 | tf_op jit(solution)/shard_map/expert_forward/pallas_call | solution.py:225
  99.0 10.5 %expert_backward.2 = (bf16[512,2048]{1,0:T(8,128)(2,1)}, bf16[512,704]{1,0:T(8,128)(2,1)}, bf16[512,704]{1,0:T(8,128)(2,1)}, f32[512,128]{1,0:T(8,128)}, bf16[70...) custom-call(bf16[512,2048]{1,0:T(8,128)(2,1)S(1)} %collective-permute-done.2.gr.x1_ref, ...), custom_call_target="tpu_custom_call" | custom-call | flops 4429185024 | bytes 17039360 | tf_op jit(solution)/shard_map/expert_backward/pallas_call | solution.py:301
  120.3 9.2 %expert_forward.3 = (bf16[512,2048]{1,0:T(8,128)(2,1)S(1)}, bf16[512,704]{1,0:T(8,128)(2,1)}, bf16[512,704]{1,0:T(8,128)(2,1)}, bf16[512,704]{1,0:T(8,128)(2,1)}, f32[512,128]{1,0:T(8,128)}, /*index=5*/f32[8,2048]{1,0:T(8,128)}) custom-call(bf16[512,2176]{1,0:T(8,128)(2,1)} %bitcast.36, bf16[704,2048]{1,0:T(8,128)(2,1)S(1)} %copy-done.15, ...), custom_call_target="tpu_custom_call" | custom-call | flops 4429185024 | bytes 17039360 | tf_op jit(solution)/shard_map/expert_forward/pallas_call | solution.py:225
  136.3 8.5 %expert_backward.3 = (bf16[512,2048]{1,0:T(8,128)(2,1)S(1)}, bf16[512,704]{1,0:T(8,128)(2,1)}, bf16[512,704]{1,0:T(8,128)(2,1)}, f32[512,128]{1,0:T(8,128)}) custom-call(bf16[512,2048]{1,0:T(8,128)(2,1)} %bitcast.13.gr.x0_ref, bf16[512,704]{1,0:T(8,128)(2,1)} %get-tuple-element.42.hg.d0_ref, bf16[512,704]{1,0:T(8,128)(2,1)} %get-tuple-element.43.fg, ...), custom_call_target="tpu_custom_call" | custom-call | flops 4429185024 | bytes 17039360 | tf_op jit(solution)/shard_map/expert_backward/pallas_call | solution.py:301
  144.7 5.1 %join_back.1 = bf16[512,2432]{1,0:T(8,128)(2,1)} custom-call(bf16[512,2048]{1,0:T(8,128)(2,1)S(1)} %get-tuple-element.51.mine_ref, bf16[512,2048]{1,0:T(8,128)(2,1)S(1)} %collective-permute-done.3.sib_ref, f32[512,128]{1,0:T(8,128)} %get-tuple-element.53.gg_ref, f32[512,128]{1,0:T(8,128)S(1)} %collective-permute-done.4.gg_sib_ref, ...), custom_call_target="tpu_custom_call" | custom-call | flops 10485760 | bytes 8388608 | tf_op jit(solution)/shard_map/join_back/pallas_call | solution.py:401
  149.8 6.2 %all-to-all-start.3 = ((bf16[64,8,2432]{2,1,0:T(8,128)(2,1)}), bf16[64,8,2432]{2,1,0:T(8,128)(2,1)S(1)}, u32[]{:S(2)}, u32[]{:S(2)}) async-start(bf16[64,8,2432]{2,1,0:T(8,128)(2,1)} %bitcast.34), calls=%async_computation.3 | async-start | bytes 4980736 | tf_op jit(solution)/shard_map/all_to_all | solution.py:555
  156.4 4.1 %collective-permute-done.1.sib_ref = bf16[512,2048]{1,0:T(8,128)(2,1)S(1)} collective-permute-done((bf16[512,2048]{1,0:T(8,128)(2,1)}, bf16[512,2048]{1,0:T(8,128)(2,1)S(1)}, u32[]{:S(2)}, u32[]{:S(2)}) %collective-permute-start.1) | collective-permute-done | bytes 2097184 | tf_op jit(solution)/shard_map/ppermute | solution.py:550
  162.1 2.0 join_halves.1
  164.1 24.0 %all-to-all-done.3 = bf16[64,8,2432]{2,1,0:T(8,128)(2,1)S(1)} async-done(((bf16[64,8,2432]{2,1,0:T(8,128)(2,1)}), bf16[64,8,2432]{2,1,0:T(8,128)(2,1)S(1)}, u32[]{:S(2)}, u32[]{:S(2)}) %all-to-all-start.3) | async-done | bytes 2490400 | tf_op jit(solution)/shard_map/all_to_all | solution.py:555
  188.1 9.5 %all-to-all-start.1 = ((bf16[64,8,2048]{2,1,0:T(8,128)(2,1)}), bf16[64,8,2048]{2,1,0:T(8,128)(2,1)}, u32[]{:S(2)}, u32[]{:S(2)}) async-start(bf16[64,8,2048]{2,1,0:T(8,128)(2,1)} %bitcast.40), calls=%async_computation.1 | async-start | bytes 4194304 | tf_op jit(solution)/shard_map/all_to_all | solution.py:555
  197.7 7.0 %shard_map.137 = bf16[704,2048]{1,0:T(8,128)(2,1)} custom-call(bf16[512,704]{1,0:T(8,128)(2,1)} %get-tuple-element.42.hg.d0_ref, bf16[512,704]{1,0:T(8,128)(2,1)} %get-tuple-element.45.hg.d1_ref, bf16[512,2048]{1,0:T(8,128)(2,1)} %bitcast.13.gr.x0_ref, bf16[512,2048]{1,0:T(8,128)(2,1)} %copy-done.7), custom_call_target="tpu_custom_call" | custom-call | flops 2952790016 | bytes 7077888 | tf_op jit(solution)/shard_map/pallas_call | solution.py:347
  204.7 7.0 %shard_map.135 = bf16[704,2048]{1,0:T(8,128)(2,1)} custom-call(bf16[512,704]{1,0:T(8,128)(2,1)} %get-tuple-element.59.d0_ref, bf16[512,704]{1,0:T(8,128)(2,1)} %get-tuple-element.60.d1_ref, bf16[512,2176]{1,0:T(8,128)(2,1)} %bitcast.38, bf16[512,2176]{1,0:T(8,128)(2,1)} %copy-done.6), custom_call_target="tpu_custom_call" | custom-call | flops 2952790016 | bytes 7077888 | tf_op jit(solution)/shard_map/pallas_call | solution.py:347
  213.9 7.0 %shard_map.136 = bf16[704,2048]{1,0:T(8,128)(2,1)} custom-call(bf16[512,704]{1,0:T(8,128)(2,1)} %get-tuple-element.61.d0_ref, bf16[512,704]{1,0:T(8,128)(2,1)} %get-tuple-element.62.d1_ref, bf16[512,2176]{1,0:T(8,128)(2,1)} %bitcast.39, bf16[512,2176]{1,0:T(8,128)(2,1)} %copy-done.6), custom_call_target="tpu_custom_call" | custom-call | flops 2952790016 | bytes 7077888 | tf_op jit(solution)/shard_map/pallas_call | solution.py:347
  220.9 3.8 %all-to-all-done.1 = bf16[64,8,2048]{2,1,0:T(8,128)(2,1)} async-done(((bf16[64,8,2048]{2,1,0:T(8,128)(2,1)}), bf16[64,8,2048]{2,1,0:T(8,128)(2,1)}, u32[]{:S(2)}, u32[]{:S(2)}) %all-to-all-start.1) | async-done | bytes 2097184 | tf_op jit(solution)/shard_map/all_to_all | solution.py:555
  224.7 4.5 %mix_outputs.1 = bf16[128,2048]{1,0:T(8,128)(2,1)} custom-call(bf16[512,128]{1,0:T(8,128)(2,1)} %get-tuple-element.35.place_ref, bf16[512,2048]{1,0:T(8,128)(2,1)} %bitcast.11.rows_ref, bf16[128,2048]{1,0:T(8,128)(2,1)} %tok_ref.5), custom_call_target="tpu_custom_call" | custom-call | flops 268435456 | bytes 2097152 | tf_op jit(solution)/shard_map/mix_outputs/pallas_call | solution.py:486
  230.1 3.1 %finish_tokens.1 = bf16[128,2048]{1,0:T(8,128)(2,1)} custom-call(bf16[512,128]{1,0:T(8,128)(2,1)S(1)} %copy-done.4, bf16[512,2432]{1,0:T(8,128)(2,1)S(1)} %bitcast.30, bf16[128,2048]{1,0:T(8,128)(2,1)S(1)} %copy-done.2, f32[1,2048]{1,0:T(1,128)S(1)} %bitcast.32, bf16[128,2048]{1,0:T(8,128)(2,1)S(1)} %copy-done.3), custom_call_target="tpu_custom_call" | custom-call | flops 268435456 | bytes 2097152 | tf_op jit(solution)/shard_map/finish_tokens/pallas_call | solution.py:529
  (53 shorter events, 28.8 us)
Async XLA Ops:
  4.3 40.7 %all-to-all-start = ((bf16[64,8,2176]{2,1,0:T(8,128)(2,1)}), bf16[64,8,2176]{2,1,0:T(8,128)(2,1)S(1)}, u32[]{:S(2)}, u32[]{:S(2)}) async-start(bf16[64,8,2176]{2,1,0:T(8,128)(2,1)} %bitcast.42), calls=%async_computation | async-start | bytes 4456448 | tf_op jit(solution)/shard_map/all_to_all | solution.py:555
  45.0 7.8 %copy-start.20 = (bf16[64,8,2176]{2,1,0:T(8,128)(2,1)}, bf16[64,8,2176]{2,1,0:T(8,128)(2,1)S(1)}, u32[]{:S(2)}) copy-start(bf16[64,8,2176]{2,1,0:T(8,128)(2,1)S(1)} %all-to-all-done) | copy-start | bytes 6684676
  45.0 33.5 %all-to-all-start.2 = ((bf16[64,8,2048]{2,1,0:T(8,128)(2,1)}), bf16[64,8,2048]{2,1,0:T(8,128)(2,1)}, u32[]{:S(2)}, u32[]{:S(2)}) async-start(bf16[64,8,2048]{2,1,0:T(8,128)(2,1)} %bitcast.41), calls=%async_computation.2 | async-start | bytes 4194304 | tf_op jit(solution)/shard_map/all_to_all | solution.py:555
  52.8 30.1 %collective-permute-start = (bf16[512,2176]{1,0:T(8,128)(2,1)}, bf16[512,2176]{1,0:T(8,128)(2,1)S(1)}, u32[]{:S(2)}, u32[]{:S(2)}) collective-permute-start(bf16[512,2176]{1,0:T(8,128)(2,1)} %bitcast.35), channel_id=1, source_target_pairs={{0,1},{1,0},{2,3},{3,2},{4,5},{5,4},{6,7},{7,6},{8,9},{9,8},{10,11... | collective-permute-start | bytes 6684680 | tf_op jit(solution)/shard_map/ppermute | solution.py:550
  78.5 20.5 %collective-permute-start.2 = (bf16[512,2048]{1,0:T(8,128)(2,1)}, bf16[512,2048]{1,0:T(8,128)(2,1)S(1)}, u32[]{:S(2)}, u32[]{:S(2)}) collective-permute-start(bf16[512,2048]{1,0:T(8,128)(2,1)} %bitcast.13.gr.x0_ref), channel_id=1, source_target_pairs={{0,1},{1,0},{2,3},{3,2},{4,5},{5,4},{6,7},{7,6},{8,9},{9,8},{10,11... | collective-permute-start | bytes 6291464 | tf_op jit(solution)/shard_map/ppermute | solution.py:550
  82.9 11.4 %copy-start.6 = (bf16[512,2176]{1,0:T(8,128)(2,1)}, bf16[512,2176]{1,0:T(8,128)(2,1)S(1)}, u32[]{:S(2)}) copy-start(bf16[512,2176]{1,0:T(8,128)(2,1)S(1)} %collective-permute-done.x_hbm.x1_ref) | copy-start | bytes 6684676
  99.0 10.5 %copy-start.7 = (bf16[512,2048]{1,0:T(8,128)(2,1)}, bf16[512,2048]{1,0:T(8,128)(2,1)S(1)}, u32[]{:S(2)}) copy-start(bf16[512,2048]{1,0:T(8,128)(2,1)S(1)} %collective-permute-done.2.gr.x1_ref) | copy-start | bytes 6291460
  111.1 1.6 copy-start.10
  112.7 1.6 copy-start.12
  114.3 30.4 %collective-permute-start.3 = (bf16[512,2048]{1,0:T(8,128)(2,1)}, bf16[512,2048]{1,0:T(8,128)(2,1)S(1)}, u32[]{:S(2)}, u32[]{:S(2)}) collective-permute-start(bf16[512,2048]{1,0:T(8,128)(2,1)} %get-tuple-element.52), channel_id=1, source_target_pairs={{0,1},{1,0},{2,3},{3,2},{4,5},{5,4},{6,7},{7,6},{8,9},{9,8},{10,11... | collective-permute-start | bytes 6291464 | tf_op jit(solution)/shard_map/ppermute | solution.py:550
  114.3 30.4 %collective-permute-start.4 = (f32[512,128]{1,0:T(8,128)}, f32[512,128]{1,0:T(8,128)S(1)}, u32[]{:S(2)}, u32[]{:S(2)}) collective-permute-start(f32[512,128]{1,0:T(8,128)} %get-tuple-element.54), channel_id=1, source_target_pairs={{0,1},{1,0},{2,3},{3,2},{4,5},{5,4},{6,7},{7,6},{8,9},{9,8},{10,11... | collective-permute-start | bytes 786440 | tf_op jit(solution)/shard_map/ppermute | solution.py:550
  114.8 1.8 copy-start.15
  116.7 1.8 copy-start.17
  118.5 1.8 copy-start.19
  130.8 1.8 copy-start.9
  132.6 1.8 copy-start.11
  134.4 1.8 copy-start.13
  149.8 38.3 %all-to-all-start.3 = ((bf16[64,8,2432]{2,1,0:T(8,128)(2,1)}), bf16[64,8,2432]{2,1,0:T(8,128)(2,1)S(1)}, u32[]{:S(2)}, u32[]{:S(2)}) async-start(bf16[64,8,2432]{2,1,0:T(8,128)(2,1)} %bitcast.34), calls=%async_computation.3 | async-start | bytes 4980736 | tf_op jit(solution)/shard_map/all_to_all | solution.py:555
  156.0 4.5 %collective-permute-start.1 = (bf16[512,2048]{1,0:T(8,128)(2,1)}, bf16[512,2048]{1,0:T(8,128)(2,1)S(1)}, u32[]{:S(2)}, u32[]{:S(2)}) collective-permute-start(bf16[512,2048]{1,0:T(8,128)(2,1)} %get-tuple-element.41), channel_id=1, source_target_pairs={{0,1},{1,0},{2,3},{3,2},{4,5},{5,4},{6,7},{7,6},{8,9},{9,8},{10,11... | collective-permute-start | bytes 6291464 | tf_op jit(solution)/shard_map/ppermute | solution.py:550
  188.1 36.5 %all-to-all-start.1 = ((bf16[64,8,2048]{2,1,0:T(8,128)(2,1)}), bf16[64,8,2048]{2,1,0:T(8,128)(2,1)}, u32[]{:S(2)}, u32[]{:S(2)}) async-start(bf16[64,8,2048]{2,1,0:T(8,128)(2,1)} %bitcast.40), calls=%async_computation.1 | async-start | bytes 4194304 | tf_op jit(solution)/shard_map/all_to_all | solution.py:555
  212.5 20.6 %collective-permute-start.5 = (f32[72,256]{1,0:T(8,128)}, f32[72,256]{1,0:T(8,128)}, u32[]{:S(2)}, u32[]{:S(2)}) collective-permute-start(f32[72,256]{1,0:T(8,128)} %collect_sums.1.mine_ref), channel_id=1, source_target_pairs={{0,1},{1,0},{2,3},{3,2},{4,5},{5,4},{6,7},{7,6},{8,9},{9,8},{10,11... | collective-permute-start | bytes 221192 | tf_op jit(solution)/shard_map/ppermute | solution.py:550
  220.9 8.2 %copy-start.2 = (bf16[128,2048]{1,0:T(8,128)(2,1)S(1)}, bf16[128,2048]{1,0:T(8,128)(2,1)}, u32[]{:S(2)}) copy-start(bf16[128,2048]{1,0:T(8,128)(2,1)} %tok_ref.5) | copy-start | bytes 1572868
  220.9 8.3 %copy-start.3 = (bf16[128,2048]{1,0:T(8,128)(2,1)S(1)}, bf16[128,2048]{1,0:T(8,128)(2,1)}, u32[]{:S(2)}) copy-start(bf16[128,2048]{1,0:T(8,128)(2,1)} %up_ref.1) | copy-start | bytes 1572868
  220.9 8.3 %copy-start.5 = (f32[2048]{0:T(1024)S(1)}, f32[2048]{0:T(1024)}, u32[]{:S(2)}) copy-start(f32[2048]{0:T(1024)} %param.9) | copy-start | bytes 24580
  (7 other events, 10.1 us)

commit v4 on v3

--- a/solution.py
+++ b/solution.py
@@ -17,6 +17,7 @@
 BF16 = jnp.bfloat16
 EPSILON = 1e-06
 KEEPING = 51 << 20
+FINISHING = 50 << 20
 
 
 def dot_nn(a, b):
@@ -432,7 +433,7 @@
         out_shape=jax.ShapeDtypeStruct((CAP + rows // CAP, 2 * LANES), F32),
         in_specs=[lane(0), lane(1), lane(2)],
         out_specs=whole((CAP + rows // CAP, 2 * LANES)),
-        compiler_params=pltpu.CompilerParams(vmem_limit_bytes=50 << 20),
+        compiler_params=pltpu.CompilerParams(vmem_limit_bytes=FINISHING),
         cost_estimate=cost(rows * rows * LANES, 6 * rows * LANES),
         name="collect_sums",
     )(rows_in, rows_in, rows_in)
@@ -456,7 +457,7 @@
         ),
         in_specs=[VMEM, VMEM, whole(gain.shape)],
         out_specs=(whole(gain.shape), whole((rows - CAP, part))),
-        compiler_params=pltpu.CompilerParams(vmem_limit_bytes=50 << 20),
+        compiler_params=pltpu.CompilerParams(vmem_limit_bytes=FINISHING),
         cost_estimate=cost(2 * mine.size, 12 * mine.size),
         name="total_sums",
     )(in_vmem(mine), in_vmem(sib), gain)
@@ -500,49 +501,47 @@
     )(place, rows, tokens)
 
 
-def finish_kernel(place_ref, rows_ref, tok_ref, gain_ref, up_ref, out_ref, acc_ref):
-    step = pl.program_id(0)
-    part = dot_tn(place_ref[...], rows_ref[...])
-
-    @pl.when(step == 0)
-    def _():
-        acc_ref[...] = part
-
-    @pl.when(step > 0)
-    def _():
-        acc_ref[...] += part
-
-    @pl.when(step == pl.num_programs(0) - 1)
-    def _():
-        x = tok_ref[...].astype(F32)
-        inverse = lax.rsqrt(jnp.mean(x * x, axis=1, keepdims=True) + EPSILON)
-        normed = x * inverse
-        gn = acc_ref[...] * gain_ref[...]
-        out = up_ref[...].astype(F32) + inverse * (gn - normed * jnp.mean(gn * normed, axis=1, keepdims=True))
-        out_ref[...] = out.astype(BF16)
+def finish_kernel(place_ref, rows_ref, tok_ref, gain_ref, up_ref, out_ref, gn_scr):
+    width = tok_ref.shape[1]
+    part = width // CHUNKS
+    x = tok_ref[...].astype(F32)
+    inverse = lax.rsqrt(jnp.mean(x * x, axis=1, keepdims=True) + EPSILON)
+    total = jnp.zeros(inverse.shape, F32)
+    for c in range(CHUNKS):
+        cols = slice(c * part, (c + 1) * part)
+        gn = dot_tn(place_ref[...], rows_ref[:, cols]) * gain_ref[:, cols]
+        gn_scr[:, cols] = gn
+        total = total + jnp.sum(gn * (tok_ref[:, cols].astype(F32) * inverse), axis=1, keepdims=True)
+    mean = total * (1.0 / width)
+    for c in range(CHUNKS):
+        cols = slice(c * part, (c + 1) * part)
+        normed = tok_ref[:, cols].astype(F32) * inverse
+        out = up_ref[:, cols].astype(F32) + inverse * (gn_scr[:, cols] - normed * mean)
+        out_ref[:, cols] = out.astype(BF16)
 
 
 def finish(place, rows, tokens, gain, upstream):
     slots, tok_count = place.shape
     width = tokens.shape[1]
-    part = 128
     return pl.pallas_call(
         finish_kernel,
-        grid=(slots // part,),
+        grid=(1,),
         out_shape=jax.ShapeDtypeStruct((tok_count, width), BF16),
         in_specs=[
-            pl.BlockSpec((part, tok_count), lambda i: (i, 0)),
-            pl.BlockSpec((part, width), lambda i: (i, 0)),
+            whole((slots, tok_count)),
+            VMEM,
             whole((tok_count, width)),
             whole((1, width)),
             whole((tok_count, width)),
         ],
         out_specs=whole((tok_count, width)),
         scratch_shapes=[pltpu.VMEM((tok_count, width), F32)],
-        compiler_params=pltpu.CompilerParams(dimension_semantics=("arbitrary",), vmem_limit_bytes=50 << 20),
+        compiler_params=pltpu.CompilerParams(
+            dimension_semantics=("arbitrary",), vmem_limit_bytes=FINISHING
+        ),
         cost_estimate=cost(2 * slots * tok_count * width, 2 * slots * width),
         name="finish_tokens",
-    )(place, rows, tokens, gain, upstream)
+    )(place, in_vmem(rows), tokens, gain, upstream)
 
 
 def across(block, axis, bit):

time: 237 us -> 236 us (level)
  no operation moved by 1% of the time
where the time goes in v4:
time: 236 us; the launch traced here: 233 us
  Pallas kernels  83.7 us (35%)
  waiting for transfers between devices  79.9 us (34%)
  starting transfers between devices  44.5 us (19%)
  local copies, waits for them, and re-layouts  24.2 us (10%)
    all_to_all x4, waiting for transfers between devices, exchange(): lax.all_to_all(x.reshape(experts, -1, width), CHIPS, 0, 0, tiled=True)  75.8 us
    all_to_all x4, starting transfers between devices, exchange(): lax.all_to_all(x.reshape(experts, -1, width), CHIPS, 0, 0, tiled=True)  35.5 us
    unnamed x42, local copies, waits for them, and re-layouts  24.2 us
    pallas_call x3, Pallas kernels, weight_grad(): pl.pallas_call(weight_grad_kernel, grid=(width // part,), out_shape=jax.S...  21 us
    pallas_call x2, Pallas kernels, forward(): pl.pallas_call(forward_loading_kernel if loading else forward_kernel, gri...  20.6 us
    pallas_call x2, Pallas kernels, backward(): pl.pallas_call(backward_loading_kernel if loading else backward_kernel, g...  19 us
    ppermute x6, starting transfers between devices, across(): return lax.ppermute(block, axis, [(i, i ^ bit) for i in range(count)])  9.05 us
    pallas_call x1, Pallas kernels, join_back(): pl.pallas_call(join_kernel, grid=(chunks + 1,), out_shape=jax.ShapeDtypeS...  5.1 us
  transfers between devices with their start and end apart: 10, of which 5 were waited for; matrix products, arithmetic and copies ran while one was open for 0% of the time, Pallas kernels for 27%

profile of v4, /device:TPU:1, one launch (start us, length us, event | category | flops | bytes accessed | tf_op | source)
XLA Modules:
  0.0 233.1 jit_solution(17918836746993762953)
XLA Ops:
  0.6 3.6 %dispatch_tokens.1 = (bf16[512,2176]{1,0:T(8,128)(2,1)}, bf16[512,128]{1,0:T(8,128)(2,1)}) custom-call(bf16[128,2048]{1,0:T(8,128)(2,1)} %tok_ref.5, f32[1,2048]{1,0:T(1,128)} %bitcast.31, s32[3,128]{1,0:T(4,128)} %bitcast.52, bf16[64,256]{1,0:T(8,128)(2,1)} %bitcast.50), custom_call_target="tpu_custom_call" | custom-call | flops 268435456 | bytes 4194304 | tf_op jit(solution)/shard_map/dispatch_tokens/pallas_call | solution.py:106
  4.3 12.0 %all-to-all-start = ((bf16[64,8,2176]{2,1,0:T(8,128)(2,1)}), bf16[64,8,2176]{2,1,0:T(8,128)(2,1)S(1)}, u32[]{:S(2)}, u32[]{:S(2)}) async-start(bf16[64,8,2176]{2,1,0:T(8,128)(2,1)} %bitcast.42), calls=%async_computation | async-start | bytes 4456448 | tf_op jit(solution)/shard_map/all_to_all | solution.py:554
  16.3 4.0 %dispatch_grads.1 = bf16[512,2048]{1,0:T(8,128)(2,1)} custom-call(bf16[512,128]{1,0:T(8,128)(2,1)} %get-tuple-element.35.place_ref, bf16[128,2048]{1,0:T(8,128)(2,1)} %up_ref.1), custom_call_target="tpu_custom_call" | custom-call | flops 268435456 | bytes 4194304 | tf_op jit(solution)/shard_map/dispatch_grads/pallas_call | solution.py:131
  20.3 24.7 %all-to-all-done = bf16[64,8,2176]{2,1,0:T(8,128)(2,1)S(1)} async-done(((bf16[64,8,2176]{2,1,0:T(8,128)(2,1)}), bf16[64,8,2176]{2,1,0:T(8,128)(2,1)S(1)}, u32[]{:S(2)}, u32[]{:S(2)}) %all-to-all-start) | async-done | bytes 2228256 | tf_op jit(solution)/shard_map/all_to_all | solution.py:554
  45.0 7.8 %all-to-all-start.2 = ((bf16[64,8,2048]{2,1,0:T(8,128)(2,1)}), bf16[64,8,2048]{2,1,0:T(8,128)(2,1)}, u32[]{:S(2)}, u32[]{:S(2)}) async-start(bf16[64,8,2048]{2,1,0:T(8,128)(2,1)} %bitcast.41), calls=%async_computation.2 | async-start | bytes 4194304 | tf_op jit(solution)/shard_map/all_to_all | solution.py:554
  52.8 2.4 %collective-permute-start = (bf16[512,2176]{1,0:T(8,128)(2,1)}, bf16[512,2176]{1,0:T(8,128)(2,1)S(1)}, u32[]{:S(2)}, u32[]{:S(2)}) collective-permute-start(bf16[512,2176]{1,0:T(8,128)(2,1)} %bitcast.35), channel_id=1, source_target_pairs={{0,1},{1,0},{2,3},{3,2},{4,5},{5,4},{6,7},{7,6},{8,9},{9,8},{10,11... | collective-permute-start | bytes 6684680 | tf_op jit(solution)/shard_map/ppermute | solution.py:549
  55.2 23.3 %all-to-all-done.2 = bf16[64,8,2048]{2,1,0:T(8,128)(2,1)} async-done(((bf16[64,8,2048]{2,1,0:T(8,128)(2,1)}), bf16[64,8,2048]{2,1,0:T(8,128)(2,1)}, u32[]{:S(2)}, u32[]{:S(2)}) %all-to-all-start.2) | async-done | bytes 2097184 | tf_op jit(solution)/shard_map/all_to_all | solution.py:554
  78.5 4.4 %collective-permute-start.2 = (bf16[512,2048]{1,0:T(8,128)(2,1)}, bf16[512,2048]{1,0:T(8,128)(2,1)S(1)}, u32[]{:S(2)}, u32[]{:S(2)}) collective-permute-start(bf16[512,2048]{1,0:T(8,128)(2,1)} %bitcast.13.gr.x0_ref), channel_id=1, source_target_pairs={{0,1},{1,0},{2,3},{3,2},{4,5},{5,4},{6,7},{7,6},{8,9},{9,8},{10,11... | collective-permute-start | bytes 6291464 | tf_op jit(solution)/shard_map/ppermute | solution.py:549
  82.9 11.4 %expert_forward.2 = (bf16[512,2048]{1,0:T(8,128)(2,1)}, bf16[512,704]{1,0:T(8,128)(2,1)}, bf16[512,704]{1,0:T(8,128)(2,1)}, bf16[512,704]{1,0:T(8,128)(2,1)}, f3...) custom-call(bf16[512,2176]{1,0:T(8,128)(2,1)S(1)} %collective-permut, ...), custom_call_target="tpu_custom_call" | custom-call | flops 4429185024 | bytes 17039360 | tf_op jit(solution)/shard_map/expert_forward/pallas_call | solution.py:226
  99.0 10.5 %expert_backward.2 = (bf16[512,2048]{1,0:T(8,128)(2,1)}, bf16[512,704]{1,0:T(8,128)(2,1)}, bf16[512,704]{1,0:T(8,128)(2,1)}, f32[512,128]{1,0:T(8,128)}, bf16[70...) custom-call(bf16[512,2048]{1,0:T(8,128)(2,1)S(1)} %collective-permute-done.2.gr.x1_ref, ...), custom_call_target="tpu_custom_call" | custom-call | flops 4429185024 | bytes 17039360 | tf_op jit(solution)/shard_map/expert_backward/pallas_call | solution.py:302
  114.8 1.8 copy-done.15
  120.3 9.2 %expert_forward.3 = (bf16[512,2048]{1,0:T(8,128)(2,1)S(1)}, bf16[512,704]{1,0:T(8,128)(2,1)}, bf16[512,704]{1,0:T(8,128)(2,1)}, bf16[512,704]{1,0:T(8,128)(2,1)}, f32[512,128]{1,0:T(8,128)}, /*index=5*/f32[8,2048]{1,0:T(8,128)}) custom-call(bf16[512,2176]{1,0:T(8,128)(2,1)} %bitcast.36, bf16[704,2048]{1,0:T(8,128)(2,1)S(1)} %copy-done.15, ...), custom_call_target="tpu_custom_call" | custom-call | flops 4429185024 | bytes 17039360 | tf_op jit(solution)/shard_map/expert_forward/pallas_call | solution.py:226
  136.3 8.5 %expert_backward.3 = (bf16[512,2048]{1,0:T(8,128)(2,1)S(1)}, bf16[512,704]{1,0:T(8,128)(2,1)}, bf16[512,704]{1,0:T(8,128)(2,1)}, f32[512,128]{1,0:T(8,128)}) custom-call(bf16[512,2048]{1,0:T(8,128)(2,1)} %bitcast.13.gr.x0_ref, bf16[512,704]{1,0:T(8,128)(2,1)} %get-tuple-element.42.hg.d0_ref, bf16[512,704]{1,0:T(8,128)(2,1)} %get-tuple-element.43.fg, ...), custom_call_target="tpu_custom_call" | custom-call | flops 4429185024 | bytes 17039360 | tf_op jit(solution)/shard_map/expert_backward/pallas_call | solution.py:302
  144.7 5.1 %join_back.1 = bf16[512,2432]{1,0:T(8,128)(2,1)} custom-call(bf16[512,2048]{1,0:T(8,128)(2,1)S(1)} %get-tuple-element.51.mine_ref, bf16[512,2048]{1,0:T(8,128)(2,1)S(1)} %collective-permute-done.3.sib_ref, f32[512,128]{1,0:T(8,128)} %get-tuple-element.53.gg_ref, f32[512,128]{1,0:T(8,128)S(1)} %collective-permute-done.4.gg_sib_ref, ...), custom_call_target="tpu_custom_call" | custom-call | flops 10485760 | bytes 8388608 | tf_op jit(solution)/shard_map/join_back/pallas_call | solution.py:402
  149.8 6.2 %all-to-all-start.3 = ((bf16[64,8,2432]{2,1,0:T(8,128)(2,1)}), bf16[64,8,2432]{2,1,0:T(8,128)(2,1)S(1)}, u32[]{:S(2)}, u32[]{:S(2)}) async-start(bf16[64,8,2432]{2,1,0:T(8,128)(2,1)} %bitcast.34), calls=%async_computation.3 | async-start | bytes 4980736 | tf_op jit(solution)/shard_map/all_to_all | solution.py:554
  156.4 4.1 %collective-permute-done.1.sib_ref = bf16[512,2048]{1,0:T(8,128)(2,1)S(1)} collective-permute-done((bf16[512,2048]{1,0:T(8,128)(2,1)}, bf16[512,2048]{1,0:T(8,128)(2,1)S(1)}, u32[]{:S(2)}, u32[]{:S(2)}) %collective-permute-start.1) | collective-permute-done | bytes 2097184 | tf_op jit(solution)/shard_map/ppermute | solution.py:549
  162.1 2.0 join_halves.1
  164.1 24.0 %all-to-all-done.3 = bf16[64,8,2432]{2,1,0:T(8,128)(2,1)S(1)} async-done(((bf16[64,8,2432]{2,1,0:T(8,128)(2,1)}), bf16[64,8,2432]{2,1,0:T(8,128)(2,1)S(1)}, u32[]{:S(2)}, u32[]{:S(2)}) %all-to-all-start.3) | async-done | bytes 2490400 | tf_op jit(solution)/shard_map/all_to_all | solution.py:554
  188.1 9.5 %all-to-all-start.1 = ((bf16[64,8,2048]{2,1,0:T(8,128)(2,1)}), bf16[64,8,2048]{2,1,0:T(8,128)(2,1)}, u32[]{:S(2)}, u32[]{:S(2)}) async-start(bf16[64,8,2048]{2,1,0:T(8,128)(2,1)} %bitcast.40), calls=%async_computation.1 | async-start | bytes 4194304 | tf_op jit(solution)/shard_map/all_to_all | solution.py:554
  197.7 7.0 %shard_map.137 = bf16[704,2048]{1,0:T(8,128)(2,1)} custom-call(bf16[512,704]{1,0:T(8,128)(2,1)} %get-tuple-element.42.hg.d0_ref, bf16[512,704]{1,0:T(8,128)(2,1)} %get-tuple-element.45.hg.d1_ref, bf16[512,2048]{1,0:T(8,128)(2,1)} %bitcast.13.gr.x0_ref, bf16[512,2048]{1,0:T(8,128)(2,1)} %copy-done.7), custom_call_target="tpu_custom_call" | custom-call | flops 2952790016 | bytes 7077888 | tf_op jit(solution)/shard_map/pallas_call | solution.py:348
  204.7 7.0 %shard_map.135 = bf16[704,2048]{1,0:T(8,128)(2,1)} custom-call(bf16[512,704]{1,0:T(8,128)(2,1)} %get-tuple-element.59.d0_ref, bf16[512,704]{1,0:T(8,128)(2,1)} %get-tuple-element.60.d1_ref, bf16[512,2176]{1,0:T(8,128)(2,1)} %bitcast.38, bf16[512,2176]{1,0:T(8,128)(2,1)} %copy-done.6), custom_call_target="tpu_custom_call" | custom-call | flops 2952790016 | bytes 7077888 | tf_op jit(solution)/shard_map/pallas_call | solution.py:348
  213.9 7.0 %shard_map.136 = bf16[704,2048]{1,0:T(8,128)(2,1)} custom-call(bf16[512,704]{1,0:T(8,128)(2,1)} %get-tuple-element.61.d0_ref, bf16[512,704]{1,0:T(8,128)(2,1)} %get-tuple-element.62.d1_ref, bf16[512,2176]{1,0:T(8,128)(2,1)} %bitcast.39, bf16[512,2176]{1,0:T(8,128)(2,1)} %copy-done.6), custom_call_target="tpu_custom_call" | custom-call | flops 2952790016 | bytes 7077888 | tf_op jit(solution)/shard_map/pallas_call | solution.py:348
  220.9 3.8 %all-to-all-done.1 = bf16[64,8,2048]{2,1,0:T(8,128)(2,1)} async-done(((bf16[64,8,2048]{2,1,0:T(8,128)(2,1)}), bf16[64,8,2048]{2,1,0:T(8,128)(2,1)}, u32[]{:S(2)}, u32[]{:S(2)}) %all-to-all-start.1) | async-done | bytes 2097184 | tf_op jit(solution)/shard_map/all_to_all | solution.py:554
  224.7 4.5 %mix_outputs.1 = bf16[128,2048]{1,0:T(8,128)(2,1)} custom-call(bf16[512,128]{1,0:T(8,128)(2,1)} %get-tuple-element.35.place_ref, bf16[512,2048]{1,0:T(8,128)(2,1)} %bitcast.11.rows_ref, bf16[128,2048]{1,0:T(8,128)(2,1)} %tok_ref.5), custom_call_target="tpu_custom_call" | custom-call | flops 268435456 | bytes 2097152 | tf_op jit(solution)/shard_map/mix_outputs/pallas_call | solution.py:487
  (53 shorter events, 28.6 us)
Async XLA Ops:
  4.3 40.7 %all-to-all-start = ((bf16[64,8,2176]{2,1,0:T(8,128)(2,1)}), bf16[64,8,2176]{2,1,0:T(8,128)(2,1)S(1)}, u32[]{:S(2)}, u32[]{:S(2)}) async-start(bf16[64,8,2176]{2,1,0:T(8,128)(2,1)} %bitcast.42), calls=%async_computation | async-start | bytes 4456448 | tf_op jit(solution)/shard_map/all_to_all | solution.py:554
  45.0 7.8 %copy-start.20 = (bf16[64,8,2176]{2,1,0:T(8,128)(2,1)}, bf16[64,8,2176]{2,1,0:T(8,128)(2,1)S(1)}, u32[]{:S(2)}) copy-start(bf16[64,8,2176]{2,1,0:T(8,128)(2,1)S(1)} %all-to-all-done) | copy-start | bytes 6684676
  45.0 33.5 %all-to-all-start.2 = ((bf16[64,8,2048]{2,1,0:T(8,128)(2,1)}), bf16[64,8,2048]{2,1,0:T(8,128)(2,1)}, u32[]{:S(2)}, u32[]{:S(2)}) async-start(bf16[64,8,2048]{2,1,0:T(8,128)(2,1)} %bitcast.41), calls=%async_computation.2 | async-start | bytes 4194304 | tf_op jit(solution)/shard_map/all_to_all | solution.py:554
  52.8 30.1 %collective-permute-start = (bf16[512,2176]{1,0:T(8,128)(2,1)}, bf16[512,2176]{1,0:T(8,128)(2,1)S(1)}, u32[]{:S(2)}, u32[]{:S(2)}) collective-permute-start(bf16[512,2176]{1,0:T(8,128)(2,1)} %bitcast.35), channel_id=1, source_target_pairs={{0,1},{1,0},{2,3},{3,2},{4,5},{5,4},{6,7},{7,6},{8,9},{9,8},{10,11... | collective-permute-start | bytes 6684680 | tf_op jit(solution)/shard_map/ppermute | solution.py:549
  78.5 20.5 %collective-permute-start.2 = (bf16[512,2048]{1,0:T(8,128)(2,1)}, bf16[512,2048]{1,0:T(8,128)(2,1)S(1)}, u32[]{:S(2)}, u32[]{:S(2)}) collective-permute-start(bf16[512,2048]{1,0:T(8,128)(2,1)} %bitcast.13.gr.x0_ref), channel_id=1, source_target_pairs={{0,1},{1,0},{2,3},{3,2},{4,5},{5,4},{6,7},{7,6},{8,9},{9,8},{10,11... | collective-permute-start | bytes 6291464 | tf_op jit(solution)/shard_map/ppermute | solution.py:549
  82.9 11.4 %copy-start.6 = (bf16[512,2176]{1,0:T(8,128)(2,1)}, bf16[512,2176]{1,0:T(8,128)(2,1)S(1)}, u32[]{:S(2)}) copy-start(bf16[512,2176]{1,0:T(8,128)(2,1)S(1)} %collective-permute-done.x_hbm.x1_ref) | copy-start | bytes 6684676
  99.0 10.5 %copy-start.7 = (bf16[512,2048]{1,0:T(8,128)(2,1)}, bf16[512,2048]{1,0:T(8,128)(2,1)S(1)}, u32[]{:S(2)}) copy-start(bf16[512,2048]{1,0:T(8,128)(2,1)S(1)} %collective-permute-done.2.gr.x1_ref) | copy-start | bytes 6291460
  111.1 1.6 copy-start.10
  112.7 1.6 copy-start.12
  114.3 30.4 %collective-permute-start.3 = (bf16[512,2048]{1,0:T(8,128)(2,1)}, bf16[512,2048]{1,0:T(8,128)(2,1)S(1)}, u32[]{:S(2)}, u32[]{:S(2)}) collective-permute-start(bf16[512,2048]{1,0:T(8,128)(2,1)} %get-tuple-element.52), channel_id=1, source_target_pairs={{0,1},{1,0},{2,3},{3,2},{4,5},{5,4},{6,7},{7,6},{8,9},{9,8},{10,11... | collective-permute-start | bytes 6291464 | tf_op jit(solution)/shard_map/ppermute | solution.py:549
  114.3 30.4 %collective-permute-start.4 = (f32[512,128]{1,0:T(8,128)}, f32[512,128]{1,0:T(8,128)S(1)}, u32[]{:S(2)}, u32[]{:S(2)}) collective-permute-start(f32[512,128]{1,0:T(8,128)} %get-tuple-element.54), channel_id=1, source_target_pairs={{0,1},{1,0},{2,3},{3,2},{4,5},{5,4},{6,7},{7,6},{8,9},{9,8},{10,11... | collective-permute-start | bytes 786440 | tf_op jit(solution)/shard_map/ppermute | solution.py:549
  114.8 1.8 copy-start.15
  116.7 1.8 copy-start.17
  118.5 1.8 copy-start.19
  130.8 1.8 copy-start.9
  132.6 1.8 copy-start.11
  134.4 1.8 copy-start.13
  149.8 38.3 %all-to-all-start.3 = ((bf16[64,8,2432]{2,1,0:T(8,128)(2,1)}), bf16[64,8,2432]{2,1,0:T(8,128)(2,1)S(1)}, u32[]{:S(2)}, u32[]{:S(2)}) async-start(bf16[64,8,2432]{2,1,0:T(8,128)(2,1)} %bitcast.34), calls=%async_computation.3 | async-start | bytes 4980736 | tf_op jit(solution)/shard_map/all_to_all | solution.py:554
  156.0 4.5 %collective-permute-start.1 = (bf16[512,2048]{1,0:T(8,128)(2,1)}, bf16[512,2048]{1,0:T(8,128)(2,1)S(1)}, u32[]{:S(2)}, u32[]{:S(2)}) collective-permute-start(bf16[512,2048]{1,0:T(8,128)(2,1)} %get-tuple-element.41), channel_id=1, source_target_pairs={{0,1},{1,0},{2,3},{3,2},{4,5},{5,4},{6,7},{7,6},{8,9},{9,8},{10,11... | collective-permute-start | bytes 6291464 | tf_op jit(solution)/shard_map/ppermute | solution.py:549
  188.1 36.5 %all-to-all-start.1 = ((bf16[64,8,2048]{2,1,0:T(8,128)(2,1)}), bf16[64,8,2048]{2,1,0:T(8,128)(2,1)}, u32[]{:S(2)}, u32[]{:S(2)}) async-start(bf16[64,8,2048]{2,1,0:T(8,128)(2,1)} %bitcast.40), calls=%async_computation.1 | async-start | bytes 4194304 | tf_op jit(solution)/shard_map/all_to_all | solution.py:554
  212.5 19.0 %collective-permute-start.5 = (f32[72,256]{1,0:T(8,128)}, f32[72,256]{1,0:T(8,128)}, u32[]{:S(2)}, u32[]{:S(2)}) collective-permute-start(f32[72,256]{1,0:T(8,128)} %collect_sums.1.mine_ref), channel_id=1, source_target_pairs={{0,1},{1,0},{2,3},{3,2},{4,5},{5,4},{6,7},{7,6},{8,9},{9,8},{10,11... | collective-permute-start | bytes 221192 | tf_op jit(solution)/shard_map/ppermute | solution.py:549
  220.9 8.2 %copy-start.2 = (bf16[128,2048]{1,0:T(8,128)(2,1)S(1)}, bf16[128,2048]{1,0:T(8,128)(2,1)}, u32[]{:S(2)}) copy-start(bf16[128,2048]{1,0:T(8,128)(2,1)} %tok_ref.5) | copy-start | bytes 1572868
  220.9 8.3 %copy-start.3 = (bf16[128,2048]{1,0:T(8,128)(2,1)S(1)}, bf16[128,2048]{1,0:T(8,128)(2,1)}, u32[]{:S(2)}) copy-start(bf16[128,2048]{1,0:T(8,128)(2,1)} %up_ref.1) | copy-start | bytes 1572868
  220.9 8.3 %copy-start.5 = (f32[2048]{0:T(1024)S(1)}, f32[2048]{0:T(1024)}, u32[]{:S(2)}) copy-start(f32[2048]{0:T(1024)} %param.9) | copy-start | bytes 24580
  (7 other events, 10.1 us)
